TPU v7x, 32 devices: a whole 2x2x4 slice. The times are simulated.
32 devices in a mesh: gx: 16 (over z, y, core), gy: 2 (over x).
Axes of the slice: x: 2, y: 2, z: 4, core: 2. Of those that a mesh axis runs over, the one named last changes fastest.
Arguments:
- prior_members: float32 [64, 3, 2, 128, 256], P(None, None, None, 'gx', 'gy'), may hold values from -0.25 to 0.25
- obs_column: int32 [16, 2, 256], P('gx', 'gy'), may hold values from 0 to 1023
- obs_value: float32 [16, 2, 256], P('gx', 'gy'), may hold values from -0.3 to 0.3
- obs_precision: float32 [16, 2, 256], P('gx', 'gy'), may hold values from 20 to 400
- obs_list: int32 [16, 32, 128], P('gx', 'gy'), may hold values from 0 to 2303, as said below
- patch_count: int32 [16, 32], P('gx', 'gy'), may hold values from 1 to 128, as said below
Outputs:
- analysis: float32 [64, 3, 2, 128, 256], P(None, None, None, 'gx', 'gy')
Inputs may be any that keep to these rules, and one draw needn't show every extreme that they name: `obs_list`: entry e of a patch's list names slot e % 256 of the tile displaced by (e // 256 // 3 - 1, e // 256 % 3 - 1) tiles in (longitude, latitude) from the patch's own tile, longitude wrapping around; never a tile beyond the latitude edges. Entries at and past the patch's count are ignored. `patch_count`: counts differ strongly from tile to tile.
All inputs are finite; a program needn't handle non-finite values.
Results may differ from a plain program's by a relative error of at most 0.0003.
Values sent between devices are 32-bit elements; how exact they have to be, the bound alone decides.
A program may use at most 64 MiB of HBM per device.

v0:
```python
import jax
import jax.numpy as jnp
from jax import lax
from jax.sharding import PartitionSpec as P

CX = 8
CY = 128
TILE_WIDTH_CELLS = 8
STEPS = 3
NS_ITERS = 3


courant = 0.3
highest = lax.Precision.HIGHEST


def padded_2(x, sides, width):
    for axis, dim in sides:
        devices, length = (lax.axis_size(axis), x.shape[dim])
        up = [(i, (i + 1) % devices) for i in range(devices)]
        down = [(j, i) for i, j in up]
        last = lax.slice_in_dim(x, length - width, length, axis=dim)
        initial = lax.slice_in_dim(x, 0, width, axis=dim)
        before = lax.ppermute(last, axis, up)
        after = lax.ppermute(initial, axis, down)
        x = jnp.concatenate([before, x, after], axis=dim)
    return x


def friedrichs_step(padded):
    depths = 1.0 + padded[..., 0, :, :, :]
    momentum_x = padded[..., 1, :, :, :]
    momentum_y = padded[..., 2, :, :, :]
    pressure = 0.5 * depths * depths
    cross_flux = momentum_x * momentum_y / depths
    flux_x = jnp.stack(
        [momentum_x, momentum_x * momentum_x / depths + pressure, cross_flux], axis=-4
    )
    flux_y = jnp.stack(
        [momentum_y, cross_flux, momentum_y * momentum_y / depths + pressure], axis=-4
    )
    neighbours = (
        padded[..., 2:, 1:-1]
        + padded[..., :-2, 1:-1]
        + padded[..., 1:-1, 2:]
        + padded[..., 1:-1, :-2]
    )
    return (
        0.25 * neighbours
        - 0.5 * courant * (flux_x[..., 2:, 1:-1] - flux_x[..., :-2, 1:-1])
        - 0.5 * courant * (flux_y[..., 1:-1, 2:] - flux_y[..., 1:-1, :-2])
    )


def cut_outside(padded, patch_border):
    extent = padded.shape[-1] - 2 * patch_border
    global_rows = (
        lax.iota(jnp.int32, padded.shape[-1]) + lax.axis_index("gy") * extent - patch_border
    )
    inside = (global_rows >= 0) & (global_rows < extent * lax.axis_size("gy"))
    return padded * inside.astype(padded.dtype)


def analyse(fields, members_obs, values, precisions, offset_x, offset_y, usable):
    members = fields.shape[1]
    obs_mean = jnp.mean(members_obs, axis=1)
    obs_pert = members_obs - obs_mean[:, None, :]
    departure = values - obs_mean
    weights = usable * precisions * jnp.exp(-((offset_x / CX) ** 2) - (offset_y / CY) ** 2)
    gram_matrix = jnp.einsum(
        "bkm,bjm->bkj", obs_pert * weights[:, None, :], obs_pert, precision=highest
    )
    bounds = members - 1.0 + jnp.sum(weights * jnp.sum(obs_pert * obs_pert, axis=1), axis=1)
    identity = jnp.eye(members, dtype=jnp.float32)
    scaled = (gram_matrix + (members - 1.0) * identity) / bounds[:, None, None]
    iterate = scaled
    inverse_root = jnp.broadcast_to(identity, scaled.shape)
    for repeat in range(NS_ITERS):
        factor = 1.5 * identity - 0.5 * jnp.einsum(
            "bij,bjk->bik", inverse_root, iterate, precision=highest
        )
        iterate = jnp.einsum("bij,bjk->bik", iterate, factor, precision=highest)
        inverse_root = jnp.einsum("bij,bjk->bik", factor, inverse_root, precision=highest)
    forcing = jnp.einsum("bkm,bm->bk", obs_pert, weights * departure, precision=highest)
    half_way = jnp.einsum("bij,bj->bi", inverse_root, forcing, precision=highest)
    mean_weight = (
        jnp.einsum("bij,bj->bi", inverse_root, half_way, precision=highest) / bounds[:, None]
    )
    spread_weight = jnp.sqrt((members - 1.0) / bounds)[:, None, None] * inverse_root
    combined = spread_weight + mean_weight[:, :, None]
    field_mean = jnp.mean(fields, axis=1)
    field_pert = fields - field_mean[:, None, :]
    return field_mean[:, None, :] + jnp.einsum(
        "bif,bik->bkf", field_pert, combined, precision=highest
    )


def local(prior_members, obs_column, obs_value, obs_precision, obs_list, patch_count):
    members = prior_members.shape[0]
    levels = prior_members.shape[2]
    width_x = prior_members.shape[3]
    width_y = prior_members.shape[4]
    states = prior_members
    padded = padded_2(states, (("gx", 3), ("gy", 4)), STEPS)
    for repeat in range(STEPS):
        padded = friedrichs_step(cut_outside(padded, STEPS - repeat))
    states = padded
    layer_mean_value = jnp.mean(states[:, 0], axis=1).reshape(members, width_x * width_y)
    columns = obs_column[0, 0]
    members_obs = jnp.take(layer_mean_value, columns, axis=1)
    local_x = (columns // width_y).astype(jnp.float32)
    local_y = (columns % width_y).astype(jnp.float32)
    extras = jnp.stack([obs_value[0, 0], obs_precision[0, 0], local_x, local_y], axis=0)
    obs_info = jnp.concatenate([members_obs, extras], axis=0)[None, None]
    beside_all = padded_2(obs_info, (("gx", 0), ("gy", 1)), 1)
    info_rows = beside_all.shape[2]
    slot_total = beside_all.shape[3]
    obs_table = jnp.transpose(beside_all, (2, 0, 1, 3)).reshape(info_rows, 9 * slot_total)
    patches_x = width_x // TILE_WIDTH_CELLS
    patches_y = width_y // TILE_WIDTH_CELLS
    batch = patches_x * patches_y
    capacity = obs_list.shape[2]
    entries = obs_list.reshape(batch, capacity)
    offset = entries // slot_total
    shift_x = offset // 3 - 1
    shift_y = offset % 3 - 1
    picked = jnp.take(obs_table, entries.reshape(-1), axis=1).reshape(info_rows, batch, capacity)
    picked_obs = jnp.transpose(picked[:members], (1, 0, 2))
    patch_x = jnp.repeat(jnp.arange(patches_x, dtype=jnp.int32), patches_y)
    patch_y = jnp.tile(jnp.arange(patches_y, dtype=jnp.int32), patches_x)
    centre_x = (patch_x * TILE_WIDTH_CELLS).astype(jnp.float32) + (TILE_WIDTH_CELLS - 1) * 0.5
    centre_y = (patch_y * TILE_WIDTH_CELLS).astype(jnp.float32) + (TILE_WIDTH_CELLS - 1) * 0.5
    offset_x = (shift_x * CX).astype(jnp.float32) + picked[members + 2] - centre_x[:, None]
    offset_y = (shift_y * CY).astype(jnp.float32) + picked[members + 3] - centre_y[:, None]
    slot_range = jnp.arange(capacity, dtype=jnp.int32)
    usable = (slot_range[None, :] < patch_count.reshape(batch)[:, None]).astype(jnp.float32)
    blocks = states.reshape(
        members, 3, levels, patches_x, TILE_WIDTH_CELLS, patches_y, TILE_WIDTH_CELLS
    )
    fields = jnp.transpose(blocks, (3, 5, 0, 1, 2, 4, 6)).reshape(
        batch, members, 3 * levels * TILE_WIDTH_CELLS * TILE_WIDTH_CELLS
    )
    result = analyse(
        fields, picked_obs, picked[members], picked[members + 1], offset_x, offset_y, usable
    )
    result = result.reshape(
        patches_x, patches_y, members, 3, levels, TILE_WIDTH_CELLS, TILE_WIDTH_CELLS
    )
    return jnp.transpose(result, (2, 3, 4, 0, 5, 1, 6)).reshape(
        members, 3, levels, width_x, width_y
    )


def solution(mesh):
    return jax.shard_map(
        local,
        mesh=mesh,
        in_specs=(
            P(None, None, None, "gx", "gy"),
            P("gx", "gy", None),
            P("gx", "gy", None),
            P("gx", "gy", None),
            P("gx", "gy", None),
            P("gx", "gy"),
        ),
        out_specs=P(None, None, None, "gx", "gy"),
        check_vma=False,
    )
```

profile of v0, /device:TPU:0, one launch (start us, length us, event | category | flops | bytes accessed | tf_op | source)
XLA Modules:
  0.0 132.2 jit_solution(6726834937167842811)
XLA Ops:
  0.0 2.2 %fusion.73 = (f32[64,3,2,3,128]{4,3,2,1,0:T(4,128)S(1)}, f32[64,3,2,3,128]{4,3,2,1,0:T(4,128)S(1)}) fusion(f32[64,3,2,8,128]{4,3,2,1,0:T(8,128)} %param.6), kind=kLoop, calls=%fused_computation.170 | loop fusion | bytes 2359296 | tf_op jit(solution)/shard_map/slice | solution.py:22
  4.5 5.0 %collective-permute-start.1 = (f32[64,3,2,3,128]{4,0,3,2,1:T(8,128)}, f32[64,3,2,3,128]{4,0,3,2,1:T(8,128)}, u32[]{:S(2)}, u32[]{:S(2)}) collective-permute-start(f32[64,3,2,3,128]{4,0,3,2,1:T(8,128)} %copy.76), channel_id=1, source_target_pairs={{2,0},{4,2},{6,4},{8,6},{10,8},{12,10},{14,12},{16,14},{18,16},{20... | collective-permute-start | bytes 1769480 | tf_op jit(solution)/shard_map/ppermute | solution.py:25
  12.4 2.1 %copy.51 = f32[64,3,2,8,128]{0,4,3,2,1:T(8,128)S(1)} copy(f32[64,3,2,8,128]{4,3,2,1,0:T(8,128)} %param.6) | data formatting | bytes 3145728 | tf_op args[0]
  17.7 2.5 %copy.50 = f32[64,3,2,3,128]{0,4,3,2,1:T(8,128)} copy(f32[64,3,2,3,128]{4,0,3,2,1:T(8,128)} %collective-permute-done) | data formatting | bytes 1179648 | tf_op jit(solution)/shard_map/ppermute | solution.py:24
  20.2 2.5 %copy.52 = f32[64,3,2,3,128]{0,4,3,2,1:T(8,128)} copy(f32[64,3,2,3,128]{4,0,3,2,1:T(8,128)} %collective-permute-done.1) | data formatting | bytes 1179648 | tf_op jit(solution)/shard_map/ppermute | solution.py:25
  22.6 1.2 pad_maximum_fusion.10
  23.9 2.0 %collective-permute-start.2 = (f32[64,3,2,14,3]{0,4,3,2,1:T(4,128)S(1)}, f32[64,3,2,14,3]{0,4,3,2,1:T(4,128)S(1)}, u32[]{:S(2)}, u32[]{:S(2)}) collective-permute-start(f32[64,3,2,14,3]{0,4,3,2,1:T(4,128)S(1)} %get-tuple-element.18), channel_id=1, source_target_pairs={{0,1},{1,0},{2,3},{3,2},{4,5},{5,4},{6,7},{7,6},{8,9},{9,8},{10,11... | collective-permute-start | bytes 193544 | tf_op jit(solution)/shard_map/ppermute | solution.py:24
  26.0 3.6 %collective-permute-done.2 = f32[64,3,2,14,3]{0,4,3,2,1:T(4,128)S(1)} collective-permute-done((f32[64,3,2,14,3]{0,4,3,2,1:T(4,128)S(1)}, f32[64,3,2,14,3]{0,4,3,2,1:T(4,128)S(1)}, u32[]{:S(2)}, u32[]{:S(2)}) %collective-permute-start.2) | collective-permute-done | bytes 64544 | tf_op jit(solution)/shard_map/ppermute | solution.py:24
  29.6 3.7 %collective-permute-done.3 = f32[64,3,2,14,3]{0,4,3,2,1:T(4,128)S(1)} collective-permute-done((f32[64,3,2,14,3]{0,4,3,2,1:T(4,128)S(1)}, f32[64,3,2,14,3]{0,4,3,2,1:T(4,128)S(1)}, u32[]{:S(2)}, u32[]{:S(2)}) %collective-permute-start.3) | collective-permute-done | bytes 64544 | tf_op jit(solution)/shard_map/ppermute | solution.py:25
  33.2 1.3 maximum_multiply_fusion
  35.4 4.7 %pad_maximum_fusion = (f32[64,3,2,14,134]{0,4,3,2,1:T(8,128)}, f32[64,3,2,14,134]{0,4,3,2,1:T(8,128)}) fusion(f32[64,1,2,14,134]{0,4,3,2,1:T(8,128)S(1)} %get-tuple-element.15, f32[64,1,2,14,134]{0,4,3,2,1:T(8,128)S(1)} %get-tuple-element.17, f32[64,1,2,14,134]{0,4,3,2,1:T(8,128)S(1)} %get-tuple-element.13, f32[64,1,2,14,134]{0,4,3,2,1:T(8,128)S(1)} %get-tuple-element.14, ...), kind=kLoop, calls=%fused_computation.3 | loop fusion | flops 2881536 | bytes 10565632 | tf_op jit(solution)/shard_map/stack | solution.py:36
  40.1 9.3 %fusion.2 = f32[64,3,2,12,132]{0,4,3,2,1:T(8,128)S(1)} fusion(f32[64,3,2,14,134]{0,4,3,2,1:T(8,128)} %get-tuple-element.31, f32[64,3,2,14,134]{0,4,3,2,1:T(8,128)} %get-tuple-element.30, f32[64,3,2,14,134]{0,4,3,2,1:T(8,128)S(1)} %maximum_multiply_fusion, f32[132]{0:T(256)S(1)} %and_convert_fusion.1), kind=kLoop, calls=%fused_computation.8 | loop fusion | flops 6690816 | bytes 21897744 | tf_op jit(solution)/shard_map/mul | solution.py:61
  50.2 2.6 %pad_maximum_fusion.2 = (f32[64,3,2,12,132]{0,4,3,2,1:T(8,128)S(1)}, f32[64,3,2,12,132]{0,4,3,2,1:T(8,128)}) fusion(f32[64,1,2,12,132]{0,4,3,2,1:T(8,128)S(1)} %get-tuple-element.22, f32[64,1,2,12,132]{0,4,3,2,1:T(8,128)S(1)} %get-tuple-element.24, f32[64,1,2,12,132]{0,4,3,2,1:T(8,128)S(1)} %get-tuple-element.20, ...), kind=kLoop, calls=%fused_computation.16 | loop fusion | flops 2433024 | bytes 8921088 | tf_op jit(solution)/shard_map/stack | solution.py:36
  52.8 6.4 %fusion.8 = f32[64,3,2,10,130]{0,4,3,2,1:T(8,128)S(1)} fusion(f32[64,3,2,12,132]{0,4,3,2,1:T(8,128)} %get-tuple-element.33, f32[64,3,2,12,132]{0,4,3,2,1:T(8,128)S(1)} %get-tuple-element.32, f32[64,3,2,12,132]{0,4,3,2,1:T(8,128)S(1)} %fusion.2, f32[130]{0:T(256)S(1)} %and_convert_fusion), kind=kLoop, calls=%fused_computation.21 | loop fusion | flops 5491200 | bytes 17971720 | tf_op jit(solution)/shard_map/mul | solution.py:61
  60.4 2.7 %bitcast_reduce_fusion.1 = (f32[16,3,2,8,8]{4,0,3,2,1:T(8,128)S(1)}, f32[64,3,2,8,128]{0,4,3,2,1:T(8,128)S(1)}) fusion(f32[64,3,2,10,130]{0,4,3,2,1:T(8,128)S(1)} %get-tuple-element.37, f32[64,3,2,10,130]{0,4,3,2,1:T(8,128)S(1)} %get-tuple-element.36, f32[64,3,2,10,130]{0,4,3,2,1:T(8,128)S(1)} %fusion.8), kind=kLoop, calls=%fused_computation.166 | loop fusion | flops 4319232 | bytes 14180352 | tf_op jit(solution)/shard_map/reduce_sum | solution.py:91
  64.1 2.5 %gather_fusion = f32[256,64]{1,0:T(8,128)} fusion(f32[64,1024]{0,1:T(8,128)} %bitcast.122, s32[1024]{0:T(1024)} %pad_clamp_fusion), kind=kCustom, calls=%fused_computation | custom fusion | bytes 132096 | tf_op jit(solution)/shard_map/jit(_take)/gather | solution.py:110
  66.6 1.7 %select_bitcast_fusion.1 = f32[64,256]{0,1:T(8,128)} fusion(f32[256,64]{1,0:T(8,128)} %gather_fusion, pred[256]{0:T(512)(128)(4,1)} %compare_and_fusion.1), kind=kLoop, calls=%fused_computation.104 | loop fusion | flops 16384 | bytes 131328 | tf_op jit(solution)/shard_map/jit(_take)/select_n | solution.py:110
  68.3 2.0 %concatenate.17 = f32[68,256]{0,1:T(8,128)} concatenate(f32[64,256]{0,1:T(8,128)} %select_bitcast_fusion.1, f32[1,256]{0,1:T(8,128)} %copy.59, f32[1,256]{0,1:T(8,128)} %copy.60, f32[1,256]{0,1:T(8,128)} %get-tuple-element.39, f32[1,256]{0,1:T(8,128)} %get-tuple-element.38), dimensions={0} | concatenate | bytes 139264 | tf_op jit(solution)/shard_map/concatenate | solution.py:114
  70.3 1.5 %collective-permute-start.4 = (f32[1,1,68,256]{2,3,1,0:T(8,128)}, f32[1,1,68,256]{2,3,1,0:T(8,128)}, u32[]{:S(2)}, u32[]{:S(2)}) collective-permute-start(f32[1,1,68,256]{2,3,1,0:T(8,128)} %bitcast.123), channel_id=1, source_target_pairs={{0,2},{2,4},{4,6},{6,8},{8,10},{10,12},{12,14},{14,16},{16,18},{18... | collective-permute-start | bytes 208904 | tf_op jit(solution)/shard_map/ppermute | solution.py:24
  71.8 3.0 %collective-permute-start.5 = (f32[1,1,68,256]{2,3,1,0:T(8,128)}, f32[1,1,68,256]{2,3,1,0:T(8,128)}, u32[]{:S(2)}, u32[]{:S(2)}) collective-permute-start(f32[1,1,68,256]{2,3,1,0:T(8,128)} %bitcast.124), channel_id=1, source_target_pairs={{2,0},{4,2},{6,4},{8,6},{10,8},{12,10},{14,12},{16,14},{18,16},{20... | collective-permute-start | bytes 208904 | tf_op jit(solution)/shard_map/ppermute | solution.py:25
  75.2 2.1 %copy.62 = f32[1,16,64,3,2,8,8]{2,6,5,4,3,1,0:T(8,128)} copy(f32[1,16,64,3,2,8,8]{2,6,1,5,4,3,0:T(8,128)S(1)} %bitcast.118) | data formatting | bytes 3145728 | tf_op jit(solution)/shard_map/transpose | solution.py:140
  77.3 2.4 %copy.63 = f32[16,64,384]{2,1,0:T(8,128)S(1)} copy(f32[16,64,384]{1,2,0:T(8,128)} %bitcast.119) | data formatting | bytes 3145728 | tf_op jit(solution)/shard_map/reshape | solution.py:140
  80.9 2.2 %collective-permute-start.6 = (f32[3,1,68,256]{2,3,1,0:T(8,128)S(1)}, f32[3,1,68,256]{2,3,1,0:T(8,128)S(1)}, u32[]{:S(2)}, u32[]{:S(2)}) collective-permute-start(f32[3,1,68,256]{2,3,1,0:T(8,128)S(1)} %pad_maximum_fusion.7), channel_id=1, source_target_pairs={{0,1},{1,0},{2,3},{3,2},{4,5},{5,4},{6,7},{7,6},{8,9},{9,8},{10,11... | collective-permute-start | bytes 626696 | tf_op jit(solution)/shard_map/ppermute | solution.py:24
  83.9 9.2 %collective-permute-done.6 = f32[3,1,68,256]{2,3,1,0:T(8,128)S(1)} collective-permute-done((f32[3,1,68,256]{2,3,1,0:T(8,128)S(1)}, f32[3,1,68,256]{2,3,1,0:T(8,128)S(1)}, u32[]{:S(2)}, u32[]{:S(2)}) %collective-permute-start.6) | collective-permute-done | bytes 208928 | tf_op jit(solution)/shard_map/ppermute | solution.py:24
  93.0 6.4 %collective-permute-done.7 = f32[3,1,68,256]{2,3,1,0:T(8,128)} collective-permute-done((f32[3,1,68,256]{2,3,1,0:T(8,128)S(1)}, f32[3,1,68,256]{2,3,1,0:T(8,128)}, u32[]{:S(2)}, u32[]{:S(2)}) %collective-permute-start.7) | collective-permute-done | bytes 208928 | tf_op jit(solution)/shard_map/ppermute | solution.py:25
  100.6 7.6 %gather_fusion.1 = f32[2048,68]{1,0:T(8,128)} fusion(f32[68,2304]{0,1:T(8,128)S(1)} %bitcast.117, s32[2048]{0:T(1024)S(1)} %broadcast_clamp_fusion), kind=kCustom, calls=%fused_computation.1 | custom fusion | bytes 1122304 | tf_op jit(solution)/shard_map/jit(_take)/gather | solution.py:127
  108.3 1.6 %select_bitcast_fusion = f32[68,2048]{0,1:T(8,128)S(1)} fusion(f32[2048,68]{1,0:T(8,128)} %gather_fusion.1, pred[2048]{0:T(1024)(128)(4,1)S(1)} %copy-done.8), kind=kLoop, calls=%fused_computation.76 | loop fusion | flops 139264 | bytes 1116160 | tf_op jit(solution)/shard_map/jit(_take)/select_n | solution.py:127
  109.9 2.3 %slice_reduce_fusion = (f32[2048]{0:T(1024)S(1)}, f32[2048]{0:T(1024)S(1)}, f32[2048]{0:T(1024)S(1)}, f32[2048]{0:T(1024)S(1)}) fusion(f32[68,2048]{0,1:T(8,128)S(1)} %select_bitcast_fusion), kind=kLoop, calls=%fused_computation.71 | loop fusion | bytes 65536 | tf_op jit(solution)/shard_map/slice | solution.py:144
  121.8 3.0 %fusion.19 = f32[16,64,384]{2,1,0:T(8,128)} fusion(f32[16,64,384]{2,1,0:T(8,128)S(1)} %copy.63, f32[16,384]{1,0:T(8,128)S(1)} %copy-done.5, f32[16,64,64]{2,1,0:T(8,128)S(1)} %fusion.77, f32[16,64]{1,0:T(8,128)S(1)} %broadcast_divide_fusion, f32[16]{0:T(128)S(1)} %get-tuple-element.41), kind=kOutput, calls=%fused_computation.55 | convolution fusion | flops 302907392 | bytes 3436608 | tf_op jit(solution)/shard_map/bif,bik->bkf/dot_general | solution.py:93
  124.8 2.1 %copy.65 = f32[16,64,384]{1,2,0:T(8,128)S(1)} copy(f32[16,64,384]{2,1,0:T(8,128)} %fusion.19) | data formatting | bytes 3145728 | tf_op jit(solution)/shard_map/add | solution.py:93
  126.9 2.1 %copy.78 = f32[64,3,2,1,8,16,8]{0,6,5,4,2,1,3:T(8,128)} copy(f32[64,3,2,1,8,16,8]{0,6,4,2,1,5,3:T(8,128)S(1)} %bitcast.120) | data formatting | bytes 3145728 | tf_op jit(solution)/shard_map/transpose | solution.py:149
  128.9 3.2 %copy.67 = f32[64,3,2,8,128]{4,3,2,1,0:T(8,128)} copy(f32[64,3,2,8,128]{0,4,3,2,1:T(8,128)} %bitcast.121) | data formatting | bytes 3145728 | tf_op jit(solution)/shard_map/reshape | solution.py:149
  (84 shorter events, 25.4 us)
Async XLA Ops:
  0.0 10.7 %copy-start.9 = (s32[1,1,256]{2,1,0:T(1,128)S(1)}, s32[1,1,256]{2,1,0:T(1,128)}, u32[]{:S(2)}) copy-start(s32[1,1,256]{2,1,0:T(1,128)} %param.7) | copy-start | bytes 3076
  0.0 11.8 %copy-start.6 = (s32[1,16,128]{2,1,0:T(8,128)S(1)}, s32[1,16,128]{2,1,0:T(8,128)}, u32[]{:S(2)}) copy-start(s32[1,16,128]{2,1,0:T(8,128)} %param.10) | copy-start | bytes 24580
  3.1 14.6 %collective-permute-start = (f32[64,3,2,3,128]{4,0,3,2,1:T(8,128)}, f32[64,3,2,3,128]{4,0,3,2,1:T(8,128)}, u32[]{:S(2)}, u32[]{:S(2)}) collective-permute-start(f32[64,3,2,3,128]{4,0,3,2,1:T(8,128)} %copy.75), channel_id=1, source_target_pairs={{0,2},{2,4},{4,6},{6,8},{8,10},{10,12},{12,14},{14,16},{16,18},{18... | collective-permute-start | bytes 1769480 | tf_op jit(solution)/shard_map/ppermute | solution.py:24
  3.6 11.0 %copy-start.10 = (f32[1,1,256]{2,1,0:T(1,128)S(1)}, f32[1,1,256]{2,1,0:T(1,128)}, u32[]{:S(2)}) copy-start(f32[1,1,256]{2,1,0:T(1,128)} %param.8) | copy-start | bytes 3076
  3.6 11.9 %copy-start.11 = (f32[1,1,256]{2,1,0:T(1,128)S(1)}, f32[1,1,256]{2,1,0:T(1,128)}, u32[]{:S(2)}) copy-start(f32[1,1,256]{2,1,0:T(1,128)} %param.9) | copy-start | bytes 3076
  4.5 15.7 %collective-permute-start.1 = (f32[64,3,2,3,128]{4,0,3,2,1:T(8,128)}, f32[64,3,2,3,128]{4,0,3,2,1:T(8,128)}, u32[]{:S(2)}, u32[]{:S(2)}) collective-permute-start(f32[64,3,2,3,128]{4,0,3,2,1:T(8,128)} %copy.76), channel_id=1, source_target_pairs={{2,0},{4,2},{6,4},{8,6},{10,8},{12,10},{14,12},{16,14},{18,16},{20... | collective-permute-start | bytes 1769480 | tf_op jit(solution)/shard_map/ppermute | solution.py:25
  22.6 10.6 %copy-start = (f32[64,3,2,3,128]{0,4,3,2,1:T(8,128)S(1)}, f32[64,3,2,3,128]{0,4,3,2,1:T(8,128)}, u32[]{:S(2)}) copy-start(f32[64,3,2,3,128]{0,4,3,2,1:T(8,128)} %copy.50) | copy-start | bytes 1769476
  22.6 10.6 %copy-start.1 = (f32[64,3,2,3,128]{0,4,3,2,1:T(8,128)S(1)}, f32[64,3,2,3,128]{0,4,3,2,1:T(8,128)}, u32[]{:S(2)}) copy-start(f32[64,3,2,3,128]{0,4,3,2,1:T(8,128)} %copy.52) | copy-start | bytes 1769476
  23.9 5.7 %collective-permute-start.2 = (f32[64,3,2,14,3]{0,4,3,2,1:T(4,128)S(1)}, f32[64,3,2,14,3]{0,4,3,2,1:T(4,128)S(1)}, u32[]{:S(2)}, u32[]{:S(2)}) collective-permute-start(f32[64,3,2,14,3]{0,4,3,2,1:T(4,128)S(1)} %get-tuple-element.18), channel_id=1, source_target_pairs={{0,1},{1,0},{2,3},{3,2},{4,5},{5,4},{6,7},{7,6},{8,9},{9,8},{10,11... | collective-permute-start | bytes 193544 | tf_op jit(solution)/shard_map/ppermute | solution.py:24
  25.9 7.4 %collective-permute-start.3 = (f32[64,3,2,14,3]{0,4,3,2,1:T(4,128)S(1)}, f32[64,3,2,14,3]{0,4,3,2,1:T(4,128)S(1)}, u32[]{:S(2)}, u32[]{:S(2)}) collective-permute-start(f32[64,3,2,14,3]{0,4,3,2,1:T(4,128)S(1)} %get-tuple-element.19), channel_id=1, source_target_pairs={{1,0},{0,1},{3,2},{2,3},{5,4},{4,5},{7,6},{6,7},{9,8},{8,9},{11,10... | collective-permute-start | bytes 193544 | tf_op jit(solution)/shard_map/ppermute | solution.py:25
  70.3 9.5 %collective-permute-start.4 = (f32[1,1,68,256]{2,3,1,0:T(8,128)}, f32[1,1,68,256]{2,3,1,0:T(8,128)}, u32[]{:S(2)}, u32[]{:S(2)}) collective-permute-start(f32[1,1,68,256]{2,3,1,0:T(8,128)} %bitcast.123), channel_id=1, source_target_pairs={{0,2},{2,4},{4,6},{6,8},{8,10},{10,12},{12,14},{14,16},{16,18},{18... | collective-permute-start | bytes 208904 | tf_op jit(solution)/shard_map/ppermute | solution.py:24
  71.8 8.1 %collective-permute-start.5 = (f32[1,1,68,256]{2,3,1,0:T(8,128)}, f32[1,1,68,256]{2,3,1,0:T(8,128)}, u32[]{:S(2)}, u32[]{:S(2)}) collective-permute-start(f32[1,1,68,256]{2,3,1,0:T(8,128)} %bitcast.124), channel_id=1, source_target_pairs={{2,0},{4,2},{6,4},{8,6},{10,8},{12,10},{14,12},{16,14},{18,16},{20... | collective-permute-start | bytes 208904 | tf_op jit(solution)/shard_map/ppermute | solution.py:25
  77.3 2.6 %copy-start.2 = (f32[68,256]{0,1:T(8,128)S(1)}, f32[68,256]{0,1:T(8,128)}, u32[]{:S(2)}) copy-start(f32[68,256]{0,1:T(8,128)} %concatenate.17) | copy-start | bytes 208900
  80.9 12.2 %collective-permute-start.6 = (f32[3,1,68,256]{2,3,1,0:T(8,128)S(1)}, f32[3,1,68,256]{2,3,1,0:T(8,128)S(1)}, u32[]{:S(2)}, u32[]{:S(2)}) collective-permute-start(f32[3,1,68,256]{2,3,1,0:T(8,128)S(1)} %pad_maximum_fusion.7), channel_id=1, source_target_pairs={{0,1},{1,0},{2,3},{3,2},{4,5},{5,4},{6,7},{7,6},{8,9},{9,8},{10,11... | collective-permute-start | bytes 626696 | tf_op jit(solution)/shard_map/ppermute | solution.py:24
  83.1 16.4 %collective-permute-start.7 = (f32[3,1,68,256]{2,3,1,0:T(8,128)S(1)}, f32[3,1,68,256]{2,3,1,0:T(8,128)}, u32[]{:S(2)}, u32[]{:S(2)}) collective-permute-start(f32[3,1,68,256]{2,3,1,0:T(8,128)S(1)} %pad_maximum_fusion.7), channel_id=1, source_target_pairs={{1,0},{0,1},{3,2},{2,3},{5,4},{4,5},{7,6},{6,7},{9,8},{8,9},{11,10... | collective-permute-start | bytes 626696 | tf_op jit(solution)/shard_map/ppermute | solution.py:25
  100.6 7.6 %copy-start.8 = (pred[2048]{0:T(1024)(128)(4,1)S(1)}, pred[2048]{0:T(1024)(128)(4,1)}, u32[]{:S(2)}) copy-start(pred[2048]{0:T(1024)(128)(4,1)} %compare_and_fusion) | copy-start | bytes 6148
  109.8 2.7 %copy-start.12 = (s32[1,16]{1,0:T(1,128)S(1)}, s32[1,16]{1,0:T(1,128)}, u32[]{:S(2)}) copy-start(s32[1,16]{1,0:T(1,128)} %param.11) | copy-start | bytes 196
  109.8 2.7 %copy-start.13 = (f32[16]{0:T(128)S(1)}, f32[16]{0:T(128)}, u32[]{:S(2)}) copy-start(f32[16]{0:T(128)} %convert_add_fusion) | copy-start | bytes 196
  109.9 3.0 %copy-start.7 = (f32[64,64]{1,0:T(8,128)S(1)}, f32[64,64]{1,0:T(8,128)}, u32[]{:S(2)}) copy-start(f32[64,64]{1,0:T(8,128)} %fusion.42) | copy-start | bytes 49156
  112.1 1.7 %copy-start.3 = (f32[64,64]{1,0:T(8,128)S(1)}, f32[64,64]{1,0:T(8,128)}, u32[]{:S(2)}) copy-start(f32[64,64]{1,0:T(8,128)} %fusion.44) | copy-start | bytes 49156
  112.1 1.7 %copy-start.4 = (f32[64,64]{1,0:T(8,128)S(1)}, f32[64,64]{1,0:T(8,128)}, u32[]{:S(2)}) copy-start(f32[64,64]{1,0:T(8,128)} %fusion.43) | copy-start | bytes 49156
  117.0 4.8 %copy-start.5 = (f32[16,384]{1,0:T(8,128)S(1)}, f32[16,384]{1,0:T(8,128)}, u32[]{:S(2)}) copy-start(f32[16,384]{1,0:T(8,128)} %copy.54) | copy-start | bytes 73732
where the time goes:
time: 133 us; the launch traced here: 132 us
  other arithmetic  42.6 us (32%)
  local copies, waits for them, and re-layouts  40.3 us (30%)
  waiting for transfers between devices  22.8 us (17%)
  starting transfers between devices  14.3 us (11%)
  matrix products  11.8 us (9%)
    mul x3, other arithmetic, cut_outside(): return padded * inside.astype(padded.dtype)  17 us
    ppermute x4, waiting for transfers between devices, padded_2(): before = lax.ppermute(last, axis, up)  12.7 us
    ppermute x4, waiting for transfers between devices, padded_2(): after = lax.ppermute(initial, axis, down)  10.1 us
    ppermute x4, starting transfers between devices, padded_2(): after = lax.ppermute(initial, axis, down)  8.14 us
    another operation x3, other arithmetic, friedrichs_step(): jnp.stack([momentum_x, momentum_x * momentum_x / depths + pressure, cross...  7.96 us
    gather x1, local copies, waits for them, and re-layouts, local(): jnp.take(obs_table, entries.reshape(-1), axis=1)  7.64 us
    ppermute x4, starting transfers between devices, padded_2(): before = lax.ppermute(last, axis, up)  6.14 us
    unnamed x31, local copies, waits for them, and re-layouts  4.02 us
  transfers between devices with their start and end apart: 8, of which 4 were waited for; matrix products, arithmetic and copies ran while one was open for 13% of the time, Pallas kernels for 0%

commit v1 on v0

v1 whole, which is shorter than its diff:
```python
import functools

import jax
import jax.numpy as jnp
from jax import lax
from jax.experimental import pallas as pl
from jax.experimental.pallas import tpu as pltpu
from jax.sharding import PartitionSpec as P

CX = 8
CY = 128
TILE_WIDTH_CELLS = 8
STEPS = 3
NS_ITERS = 3


courant = 0.3
highest = lax.Precision.HIGHEST


def padded_2(x, sides, width):
    for axis, dim in sides:
        devices, length = (lax.axis_size(axis), x.shape[dim])
        up = [(i, (i + 1) % devices) for i in range(devices)]
        down = [(j, i) for i, j in up]
        last = lax.slice_in_dim(x, length - width, length, axis=dim)
        initial = lax.slice_in_dim(x, 0, width, axis=dim)
        before = lax.ppermute(last, axis, up)
        after = lax.ppermute(initial, axis, down)
        x = jnp.concatenate([before, x, after], axis=dim)
    return x


def friedrichs_step(padded):
    depths = 1.0 + padded[..., 0, :, :, :]
    momentum_x = padded[..., 1, :, :, :]
    momentum_y = padded[..., 2, :, :, :]
    pressure = 0.5 * depths * depths
    cross_flux = momentum_x * momentum_y / depths
    flux_x = jnp.stack(
        [momentum_x, momentum_x * momentum_x / depths + pressure, cross_flux], axis=-4
    )
    flux_y = jnp.stack(
        [momentum_y, cross_flux, momentum_y * momentum_y / depths + pressure], axis=-4
    )
    neighbours = (
        padded[..., 2:, 1:-1]
        + padded[..., :-2, 1:-1]
        + padded[..., 1:-1, 2:]
        + padded[..., 1:-1, :-2]
    )
    return (
        0.25 * neighbours
        - 0.5 * courant * (flux_x[..., 2:, 1:-1] - flux_x[..., :-2, 1:-1])
        - 0.5 * courant * (flux_y[..., 1:-1, 2:] - flux_y[..., 1:-1, :-2])
    )


def cut_outside(padded, patch_border):
    extent = padded.shape[-1] - 2 * patch_border
    global_rows = (
        lax.iota(jnp.int32, padded.shape[-1]) + lax.axis_index("gy") * extent - patch_border
    )
    inside = (global_rows >= 0) & (global_rows < extent * lax.axis_size("gy"))
    return padded * inside.astype(padded.dtype)


def split(x):
    hi = x.astype(jnp.bfloat16)
    return hi, (x - hi.astype(jnp.float32)).astype(jnp.bfloat16)


def dot_nn(a, b):
    return lax.dot_general(a, b, (((1,), (0,)), ((), ())), preferred_element_type=jnp.float32)


def dot_nt(a, b):
    return lax.dot_general(a, b, (((1,), (1,)), ((), ())), preferred_element_type=jnp.float32)


def analysis_kernel(
    geometry, fields_ref, table_ref, extras_ref, list_ref, count_ref, out_ref,
    weights, gram, force, turned, combined, result_ref, done_sem,
):
    width_x, width_y, patches_x, patches_y, rows_in_y = geometry
    kinds, columns, members, lanes = fields_ref.shape
    tiles, _, slots = extras_ref.shape
    batch, capacity = list_ref.shape
    per_tile = slots // 128
    halves = kinds * columns // 2

    chunks = tiles * per_tile
    padded_chunks = -(-chunks // 8) * 8
    usable_at = lax.broadcasted_iota(jnp.int32, (1, capacity), 1)
    chunk_id = lax.broadcasted_iota(jnp.int32, (padded_chunks, capacity), 0)
    lane_id = lax.broadcasted_iota(jnp.int32, (128, capacity), 0)
    for patch in range(batch):
        named = list_ref[patch : patch + 1, :]
        usable = usable_at < count_ref[patch : patch + 1, :]
        upper = jnp.where(usable, named // 128, -1)
        lower = named % 128
        counts = dot_nt(
            (chunk_id == upper).astype(jnp.float32).astype(jnp.bfloat16),
            (lane_id == lower).astype(jnp.float32).astype(jnp.bfloat16),
        )
        for chunk in range(chunks):
            tile, part = divmod(chunk, per_tile)
            weights[tile, patch : patch + 1, part * 128 : part * 128 + 128] = counts[
                chunk : chunk + 1
            ]

    patch_id = lax.broadcasted_iota(jnp.int32, (batch, slots), 0)
    centre_x = (patch_id // patches_y * TILE_WIDTH_CELLS).astype(jnp.float32) + (
        TILE_WIDTH_CELLS - 1
    ) * 0.5
    centre_y = (patch_id % patches_y * TILE_WIDTH_CELLS).astype(jnp.float32) + (
        TILE_WIDTH_CELLS - 1
    ) * 0.5
    gram[...] = jnp.zeros_like(gram)
    force[...] = jnp.zeros_like(force)
    for tile in range(tiles):
        shift_x, shift_y = tile // 3 - 1, tile % 3 - 1

        def add_tile():
            info = extras_ref[tile]
            offset_x = shift_x * width_x + info[2:3] - centre_x
            offset_y = shift_y * width_y + info[3:4] - centre_y
            near = jnp.exp(-((offset_x / width_x) ** 2) - (offset_y / width_y) ** 2)
            factor = weights[tile] * info[1:2] * near
            values = table_ref[tile]
            mean = jnp.sum(values, axis=0, keepdims=True) / members
            pert = values - mean
            upper, lower = split(pert)
            both = jnp.concatenate([upper, lower], axis=0)
            for patch in range(batch):
                first, second = split(pert * factor[patch : patch + 1])
                gram[patch] += dot_nt(jnp.concatenate([first, second], axis=0), both)
            first, second = split(factor * (info[0:1] - mean))
            rest = jnp.zeros((128 - 2 * batch, slots), jnp.bfloat16)
            force[...] += dot_nt(both, jnp.concatenate([first, second, rest], axis=0))

        row = lax.axis_index("gy") + shift_y
        pl.when((row >= 0) & (row < rows_in_y))(add_tile)

    for half in range(halves):
        kind, column = divmod(2 * half, columns)
        pair = []
        for step in range(2):
            block = fields_ref[kind, column + step]
            pair.append(block - jnp.sum(block, axis=0, keepdims=True) / members)
        flipped = jnp.transpose(jnp.concatenate(pair, axis=0))
        for strip in range(patches_y):
            turned[strip, half * 8 : half * 8 + 8, :] = flipped[strip * 8 : strip * 8 + 8]

    ahead = 256 // members
    groups = batch // ahead
    lane128 = lax.broadcasted_iota(jnp.int32, (members, 128), 1)
    own_row = lax.broadcasted_iota(jnp.int32, (members, 128), 0)
    diagonal = lane128 % members == own_row
    on_left = lane128 < members
    identity1 = jnp.where(diagonal, 1.0, 0.0)
    identity = jnp.concatenate([identity1, identity1], axis=1)
    in_block = (
        lax.broadcasted_iota(jnp.int32, (256, 256), 0) // members
        == lax.broadcasted_iota(jnp.int32, (256, 256), 1) // members
    ).astype(jnp.float32).astype(jnp.bfloat16)

    def tiled(part):
        return jnp.concatenate([part] * ahead, axis=0) * in_block

    def left(x):
        hi, lo = split(x)
        return jnp.concatenate([hi, lo], axis=0), hi

    def right(x):
        hi, lo = split(x)
        return tiled(hi), tiled(lo)

    def product(x, y):
        both = dot_nn(x[0], y[0])
        return both[:members] + both[members:] + dot_nn(x[1], y[1])

    scaled, inverse_bounds = [], []
    for group in range(groups):
        parts, bounds = [], []
        for pair in range(ahead // 2):
            even = gram[group * ahead + 2 * pair]
            odd = gram[group * ahead + 2 * pair + 1]
            matrix = jnp.where(
                on_left,
                even[:members] + pltpu.roll(even[:members], members, 1) + even[members:],
                odd[:members]
                + pltpu.roll(odd[:members], members, 1)
                + pltpu.roll(odd[members:], members, 1),
            )
            trace = jnp.where(diagonal, matrix, 0.0)
            first = jnp.sum(jnp.where(on_left, trace, 0.0), keepdims=True)
            second = jnp.sum(jnp.where(on_left, 0.0, trace), keepdims=True)
            bounds.append(members - 1.0 + jnp.where(on_left[:1], first, second))
            parts.append(matrix)
        bounds = jnp.concatenate(bounds, axis=1)
        matrix = jnp.concatenate(parts, axis=1)
        scaled.append((matrix + (members - 1.0) * identity) / bounds)
        inverse_bounds.append(1.0 / bounds)

    iterate = [left(a) for a in scaled]
    values = scaled
    factors = [1.5 * identity - 0.5 * a for a in scaled]
    roots = factors
    for repeat in range(1, NS_ITERS):
        factor_right = [right(s) for s in factors]
        iterate = [left(v) for v in values]
        values = [product(y, s) for y, s in zip(iterate, factor_right)]
        root_left = [left(z) for z in roots]
        value_right = [right(v) for v in values]
        factors = [
            1.5 * identity - 0.5 * product(z, y) for z, y in zip(root_left, value_right)
        ]
        factor_left = [left(s) for s in factors]
        root_right = [right(z) for z in roots]
        roots = [product(s, z) for s, z in zip(factor_left, root_right)]

    total = force[...]
    forcing = (
        total[:members] + pltpu.roll(total[:members], 128 - batch, 1) + total[members:]
    )
    block_row = lax.broadcasted_iota(jnp.int32, (256, 128), 0) // members
    block_lane = lax.broadcasted_iota(jnp.int32, (256, 128), 1)
    for group in range(groups):
        root = left(roots[group])
        keep = (block_row + group * ahead == block_lane).astype(jnp.float32).astype(jnp.bfloat16)
        vector = forcing
        for repeat in range(2):
            hi, lo = split(vector)
            hi = jnp.concatenate([hi] * ahead, axis=0) * keep
            lo = jnp.concatenate([lo] * ahead, axis=0) * keep
            vector = product(root, (hi, lo))
        shift = []
        for pair in range(ahead // 2):
            first = group * ahead + 2 * pair
            shift.append(
                jnp.where(on_left, vector[:, first : first + 1], vector[:, first + 1 : first + 2])
            )
        shift = jnp.concatenate(shift, axis=1)
        inverse = inverse_bounds[group]
        whole = jnp.sqrt((members - 1.0) * inverse) * roots[group] + shift * inverse
        for pair in range(ahead // 2):
            combined[group * (ahead // 2) + pair] = whole[:, pair * 128 : pair * 128 + 128]

    for strip in range(batch):
        both = combined[strip // 2]
        other = pltpu.roll(both, members, 1)
        on_diag, off_diag = (both, other) if strip % 2 == 0 else (other, both)
        matrix = jnp.concatenate(
            [jnp.where(on_left, on_diag, 0.0), jnp.where(on_left, 0.0, off_diag)], axis=0
        )
        hi, lo = split(matrix)
        upper, lower = split(turned[strip])
        turned[strip] = dot_nn(
            jnp.concatenate([upper, lower], axis=1), jnp.concatenate([hi, hi], axis=0)
        ) + dot_nn(upper, lo)

    copies = []
    for half in range(halves):
        kind, column = divmod(2 * half, columns)
        result = jnp.transpose(
            jnp.concatenate(
                [turned[strip, half * 8 : half * 8 + 8, :] for strip in range(patches_y)], axis=0
            )
        )
        for step in range(2):
            block = fields_ref[kind, column + step]
            mean = jnp.sum(block, axis=0, keepdims=True) / members
            result_ref[kind, column + step] = (
                mean + result[step * members : step * members + members]
            )
            copies.append(
                pltpu.make_async_copy(
                    result_ref.at[kind, column + step],
                    out_ref.at[:, kind, column + step, :],
                    done_sem.at[kind * columns + column + step],
                )
            )
            copies[-1].start()
    for copy in copies:
        copy.wait()


def analyse(fields, table, extras, entries, counts, width_x, width_y):
    kinds, columns, members, lanes = fields.shape
    tiles, _, slots = extras.shape
    batch = entries.shape[0]
    geometry = (
        width_x, width_y, width_x // TILE_WIDTH_CELLS, width_y // TILE_WIDTH_CELLS,
        lax.axis_size("gy"),
    )
    vmem = pl.BlockSpec(memory_space=pltpu.VMEM)
    return pl.pallas_call(
        functools.partial(analysis_kernel, geometry),
        out_shape=jax.ShapeDtypeStruct((members, kinds, columns, lanes), jnp.float32),
        in_specs=[vmem] * 5,
        out_specs=pl.BlockSpec(memory_space=pl.ANY),
        scratch_shapes=[
            pltpu.VMEM((tiles, batch, slots), jnp.float32),
            pltpu.VMEM((batch, 2 * members, 2 * members), jnp.float32),
            pltpu.VMEM((2 * members, 128), jnp.float32),
            pltpu.VMEM((batch, kinds * columns // 2 * 8, 128), jnp.float32),
            pltpu.VMEM((batch // 2, members, 128), jnp.float32),
            pltpu.VMEM(fields.shape, jnp.float32),
            pltpu.SemaphoreType.DMA((kinds * columns,)),
        ],
        compiler_params=pltpu.CompilerParams(vmem_limit_bytes=40 << 20),
    )(fields, table, extras, entries, counts)


def local(prior_members, obs_column, obs_value, obs_precision, obs_list, patch_count):
    members = prior_members.shape[0]
    levels = prior_members.shape[2]
    width_x = prior_members.shape[3]
    width_y = prior_members.shape[4]
    states = prior_members
    padded = padded_2(states, (("gx", 3), ("gy", 4)), STEPS)
    for repeat in range(STEPS):
        padded = friedrichs_step(cut_outside(padded, STEPS - repeat))
    states = padded
    layer_mean_value = jnp.mean(states[:, 0], axis=1).reshape(members, width_x * width_y)
    columns = obs_column[0, 0]
    members_obs = jnp.take(layer_mean_value, columns, axis=1)
    local_x = (columns // width_y).astype(jnp.float32)
    local_y = (columns % width_y).astype(jnp.float32)
    extras = jnp.stack([obs_value[0, 0], obs_precision[0, 0], local_x, local_y], axis=0)
    obs_info = jnp.concatenate([members_obs, extras], axis=0)[None, None]
    beside_all = padded_2(obs_info, (("gx", 0), ("gy", 1)), 1)
    info_rows, slot_total = beside_all.shape[2:]
    everything = beside_all.reshape(9, info_rows, slot_total)
    fields = jnp.transpose(states, (1, 2, 3, 0, 4)).reshape(
        3 * levels, width_x, members, width_y
    )
    batch = obs_list.shape[0] * obs_list.shape[1]
    result = analyse(
        fields,
        everything[:, :members],
        everything[:, members:],
        obs_list.reshape(batch, obs_list.shape[2]),
        patch_count.reshape(batch, 1),
        width_x,
        width_y,
    )
    return result.reshape(members, 3, levels, width_x, width_y)


def solution(mesh):
    return jax.shard_map(
        local,
        mesh=mesh,
        in_specs=(
            P(None, None, None, "gx", "gy"),
            P("gx", "gy", None),
            P("gx", "gy", None),
            P("gx", "gy", None),
            P("gx", "gy", None),
            P("gx", "gy"),
        ),
        out_specs=P(None, None, None, "gx", "gy"),
        check_vma=False,
    )
```

time: 133 us -> 143 us (1.075)
  other arithmetic: 42.6 us -> 88 us
  local copies, waits for them, and re-layouts: 40.3 us -> 20.2 us
  matrix products: 11.8 us -> 0 us
  waiting for transfers between devices: 22.8 us -> 11.1 us
  Pallas kernels: 0 us -> 8.33 us
    mul x3, other arithmetic: 17 us -> 36.8 us  [cut_outside(): return padded * inside.astype(padded.dtype)]
    transpose x0 -> x1, other arithmetic: none -> 17.6 us  [local(): jnp.transpose(states, (1, 2, 3, 0, 4))]
    dot_general x13 -> x0, matrix products: 11.8 us -> none  [the longest x1 3 us: analyse(): jnp.einsum('bif,bik->bkf', field_pert, combined, precision=highest)]
    sub x0 -> x1, other arithmetic: none -> 10.3 us  [friedrichs_step(): 0.25 * neighbours]
    pallas_call x0 -> x1, Pallas kernels: none -> 8.33 us  [analyse(): pl.pallas_call(functools.partial(analysis_kernel, geometry), out_shape=ja...]
    gather x1 -> x0, local copies, waits for them, and re-layouts: 7.64 us -> none  [local(): jnp.take(obs_table, entries.reshape(-1), axis=1)]
    ppermute x4, waiting for transfers between devices: 10.1 us -> 2.61 us  [padded_2(): after = lax.ppermute(initial, axis, down)]
    slice x3, other arithmetic: 2.22 us -> 8.97 us  [friedrichs_step(): momentum_x = padded[..., 1, :, :, :]]
  transfers between devices with their start and end apart: 8 -> 8, of which waited for: 4 -> 4; matrix products, arithmetic and copies ran while one was open for 13% -> 19% of each run, Pallas kernels for 0% -> 0%
where the time goes in v1:
time: 143 us; the launch traced here: 142 us
  other arithmetic  88 us (62%)
  local copies, waits for them, and re-layouts  20.2 us (14%)
  starting transfers between devices  14.2 us (10%)
  waiting for transfers between devices  11.1 us (8%)
  Pallas kernels  8.33 us (6%)
    mul x3, other arithmetic, cut_outside(): return padded * inside.astype(padded.dtype)  36.8 us
    transpose x1, other arithmetic, local(): jnp.transpose(states, (1, 2, 3, 0, 4))  17.6 us
    another operation x2, other arithmetic, friedrichs_step(): jnp.stack([momentum_x, momentum_x * momentum_x / depths + pressure, cross...  10.6 us
    sub x1, other arithmetic, friedrichs_step(): 0.25 * neighbours  10.3 us
    slice x3, other arithmetic, friedrichs_step(): momentum_x = padded[..., 1, :, :, :]  8.97 us
    ppermute x4, waiting for transfers between devices, padded_2(): before = lax.ppermute(last, axis, up)  8.5 us
    pallas_call x1, Pallas kernels, analyse(): pl.pallas_call(functools.partial(analysis_kernel, geometry), out_shape=ja...  8.33 us
    ppermute x4, starting transfers between devices, padded_2(): after = lax.ppermute(initial, axis, down)  7.8 us
  transfers between devices with their start and end apart: 8, of which 4 were waited for; matrix products, arithmetic and copies ran while one was open for 19% of the time, Pallas kernels for 0%

profile of v1, /device:TPU:0, one launch (start us, length us, event | category | flops | bytes accessed | tf_op | source)
XLA Modules:
  0.0 142.2 jit_solution(8574181280966093941)
XLA Ops:
  0.0 2.2 %fusion.26 = (f32[64,3,2,3,128]{4,3,2,1,0:T(4,128)S(1)}, f32[64,3,2,3,128]{4,3,2,1,0:T(4,128)S(1)}) fusion(f32[64,3,2,8,128]{4,3,2,1,0:T(8,128)} %param.6), kind=kLoop, calls=%fused_computation.85 | loop fusion | bytes 2359296 | tf_op jit(solution)/shard_map/slice | solution.py:26
  2.2 0.9 copy.69
  3.7 0.9 copy.70
  4.6 5.0 %collective-permute-start.1 = (f32[64,3,2,3,128]{4,0,3,2,1:T(8,128)}, f32[64,3,2,3,128]{4,0,3,2,1:T(8,128)}, u32[]{:S(2)}, u32[]{:S(2)}) collective-permute-start(f32[64,3,2,3,128]{4,0,3,2,1:T(8,128)} %copy.70), channel_id=1, source_target_pairs={{2,0},{4,2},{6,4},{8,6},{10,8},{12,10},{14,12},{16,14},{18,16},{20... | collective-permute-start | bytes 1769480 | tf_op jit(solution)/shard_map/ppermute | solution.py:29
  9.6 2.3 %copy.55 = f32[64,3,2,8,128]{0,3,4,2,1:T(8,128)S(1)} copy(f32[64,3,2,8,128]{4,3,2,1,0:T(8,128)} %param.6) | data formatting | bytes 3145728 | tf_op args[0]
  13.8 2.8 %collective-permute-done = f32[64,3,2,3,128]{4,0,3,2,1:T(8,128)} collective-permute-done((f32[64,3,2,3,128]{4,0,3,2,1:T(8,128)}, f32[64,3,2,3,128]{4,0,3,2,1:T(8,128)}, u32[]{:S(2)}, u32[]{:S(2)}) %collective-permute-start) | collective-permute-done | bytes 589856 | tf_op jit(solution)/shard_map/ppermute | solution.py:28
  16.6 2.4 %copy.54 = f32[64,3,2,3,128]{0,3,4,2,1:T(4,128)} copy(f32[64,3,2,3,128]{4,0,3,2,1:T(8,128)} %collective-permute-done) | data formatting | bytes 1179648 | tf_op jit(solution)/shard_map/ppermute | solution.py:28
  19.0 2.4 %copy.56 = f32[64,3,2,3,128]{0,3,4,2,1:T(4,128)} copy(f32[64,3,2,3,128]{4,0,3,2,1:T(8,128)} %collective-permute-done.1) | data formatting | bytes 1179648 | tf_op jit(solution)/shard_map/ppermute | solution.py:29
  21.4 1.0 pad_maximum_fusion.12
  22.5 2.0 %collective-permute-start.2 = (f32[64,3,2,14,3]{0,3,4,2,1:T(8,128)S(1)}, f32[64,3,2,14,3]{0,3,4,2,1:T(8,128)S(1)}, u32[]{:S(2)}, u32[]{:S(2)}) collective-permute-start(f32[64,3,2,14,3]{0,3,4,2,1:T(8,128)S(1)} %get-tuple-element.20), channel_id=1, source_target_pairs={{0,1},{1,0},{2,3},{3,2},{4,5},{5,4},{6,7},{7,6},{8,9},{9,8},{10,11... | collective-permute-start | bytes 193544 | tf_op jit(solution)/shard_map/ppermute | solution.py:28
  24.6 3.1 %collective-permute-done.2 = f32[64,3,2,14,3]{0,3,4,2,1:T(8,128)S(1)} collective-permute-done((f32[64,3,2,14,3]{0,3,4,2,1:T(8,128)S(1)}, f32[64,3,2,14,3]{0,3,4,2,1:T(8,128)S(1)}, u32[]{:S(2)}, u32[]{:S(2)}) %collective-permute-start.2) | collective-permute-done | bytes 64544 | tf_op jit(solution)/shard_map/ppermute | solution.py:28
  27.7 2.6 %collective-permute-done.3 = f32[64,3,2,14,3]{0,3,4,2,1:T(8,128)S(1)} collective-permute-done((f32[64,3,2,14,3]{0,3,4,2,1:T(8,128)S(1)}, f32[64,3,2,14,3]{0,3,4,2,1:T(8,128)S(1)}, u32[]{:S(2)}, u32[]{:S(2)}) %collective-permute-start.3) | collective-permute-done | bytes 64544 | tf_op jit(solution)/shard_map/ppermute | solution.py:29
  30.3 3.7 %maximum_multiply_fusion = f32[64,3,2,14,134]{0,3,4,2,1:T(8,128)S(1)} fusion(f32[64,3,2,14,3]{0,3,4,2,1:T(8,128)S(1)} %collective-permute-done.3, f32[64,3,2,3,128]{0,3,4,2,1:T(4,128)S(1)} %copy-done.4, f32[64,3,2,8,128]{0,3,4,2,1:T(8,128)S(1)} %copy.55, f32[64,3,2,3,128]{0,3,4,2,1:T(4,128)S(1)} %copy-done.3, ...), kind=kLoop, calls=%fused_computation.1 | loop fusion | flops 3601920 | bytes 5763608 | tf_op jit(solution)/shard_map/mul | solution.py:65
  34.0 0.9 fusion.23
  34.9 5.4 %pad_maximum_fusion = (f32[64,3,2,14,134]{0,3,4,2,1:T(8,128)}, f32[64,3,2,14,134]{0,3,4,2,1:T(8,128)}) fusion(f32[64,1,2,14,134]{0,3,4,2,1:T(8,128)S(1)} %get-tuple-element.7, f32[64,1,2,14,134]{0,3,4,2,1:T(8,128)S(1)} %get-tuple-element.9, f32[64,1,2,14,134]{0,3,4,2,1:T(8,128)S(1)} %get-tuple-element.5, f32[64,1,2,14,134]{0,3,4,2,1:T(8,128)S(1)} %get-tuple-element.6, ...), kind=kLoop, calls=%fused_computation.2 | loop fusion | flops 2881536 | bytes 10565632 | tf_op jit(solution)/shard_map/stack | solution.py:40
  40.3 11.6 %fusion.2 = f32[64,3,2,12,132]{0,3,4,2,1:T(8,128)S(1)} fusion(f32[64,3,2,14,134]{0,3,4,2,1:T(8,128)} %get-tuple-element.23, f32[64,3,2,14,134]{0,3,4,2,1:T(8,128)} %get-tuple-element.22, f32[64,3,2,14,134]{0,3,4,2,1:T(8,128)S(1)} %maximum_multiply_fusion, f32[132]{0:T(256)S(1)} %and_convert_fusion.1), kind=kLoop, calls=%fused_computation.7 | loop fusion | flops 6690816 | bytes 21897744 | tf_op jit(solution)/shard_map/mul | solution.py:65
  51.8 1.1 fusion.24
  53.0 2.0 %copy-done.1 = f32[64,3,2,12,132]{0,3,4,2,1:T(8,128)} copy-done((f32[64,3,2,12,132]{0,3,4,2,1:T(8,128)}, f32[64,3,2,12,132]{0,3,4,2,1:T(8,128)S(1)}, u32[]{:S(2)}) %copy-start.1) | copy-done | bytes 2433048
  54.9 5.2 %pad_maximum_fusion.2 = (f32[64,3,2,12,132]{0,3,4,2,1:T(8,128)}, f32[64,3,2,12,132]{0,3,4,2,1:T(8,128)}) fusion(f32[64,1,2,12,132]{0,3,4,2,1:T(8,128)S(1)} %get-tuple-element.12, f32[64,1,2,12,132]{0,3,4,2,1:T(8,128)S(1)} %get-tuple-element.14, f32[64,1,2,12,132]{0,3,4,2,1:T(8,128)S(1)} %get-tuple-element.10, ...), kind=kLoop, calls=%fused_computation.15 | loop fusion | flops 2433024 | bytes 8921088 | tf_op jit(solution)/shard_map/stack | solution.py:40
  60.1 21.5 %fusion.8 = f32[64,3,2,10,130]{0,3,4,2,1:T(8,128)} fusion(f32[64,3,2,12,132]{0,3,4,2,1:T(8,128)} %get-tuple-element.25, f32[64,3,2,12,132]{0,3,4,2,1:T(8,128)} %get-tuple-element.24, f32[64,3,2,12,132]{0,3,4,2,1:T(8,128)} %copy-done.1, f32[130]{0:T(256)S(1)} %and_convert_fusion), kind=kLoop, calls=%fused_computation.20 | loop fusion | flops 5491200 | bytes 17971720 | tf_op jit(solution)/shard_map/mul | solution.py:65
  81.7 7.0 %fusion.25 = (f32[64,1,2,10,130]{0,3,4,2,1:T(8,128)S(1)}, f32[64,1,2,10,130]{0,3,4,2,1:T(8,128)}, f32[64,1,2,10,130]{0,3,4,2,1:T(8,128)}, f32[64,1,2,10,130]{0,3,4,2,1:T(8,128)}, f32[64,1,2,10,130]{0,3,4,2,1:T(8,128)}) fusion(f32[64,3,2,10,130]{0,3,4,2,1:T(8,128)} %fusion.8), kind=kLoop, calls=%fused_computation.84 | loop fusion | flops 1830400 | bytes 5324800 | tf_op jit(solution)/shard_map/slice | solution.py:36
  88.7 10.3 %fusion.14 = f32[64,3,2,8,128]{0,3,4,2,1:T(8,128)} fusion(f32[64,1,2,10,130]{0,3,4,2,1:T(8,128)} %get-tuple-element.16, f32[64,1,2,10,130]{0,3,4,2,1:T(8,128)} %get-tuple-element.17, f32[64,1,2,10,130]{0,3,4,2,1:T(8,128)} %get-tuple-element.18, f32[64,1,2,10,130]{0,3,4,2,1:T(8,128)} %get-tuple-element.19, f32[64,1,2,10,130]{0,3,4,2,1:T(8,128)S(1)} %get-tuple-element.15, ...), kind=kLoop, calls=%fused_computation.34 | loop fusion | flops 7077888 | bytes 11192320 | tf_op jit(solution)/shard_map/sub | solution.py:53
  99.0 1.4 slice_reduce_fusion
  101.7 1.2 concatenate.17
  102.9 2.4 %collective-permute-start.4 = (f32[1,1,68,256]{2,3,1,0:T(8,128)S(1)}, f32[1,1,68,256]{2,3,1,0:T(8,128)S(1)}, u32[]{:S(2)}, u32[]{:S(2)}) collective-permute-start(f32[1,1,68,256]{2,3,1,0:T(8,128)S(1)} %bitcast.23), channel_id=1, source_target_pairs={{0,2},{2,4},{4,6},{6,8},{8,10},{10,12},{12,14},{14,16},{16,18},{18... | collective-permute-start | bytes 208904 | tf_op jit(solution)/shard_map/ppermute | solution.py:28
  105.2 2.1 %collective-permute-start.5 = (f32[1,1,68,256]{2,3,1,0:T(8,128)S(1)}, f32[1,1,68,256]{2,3,1,0:T(8,128)S(1)}, u32[]{:S(2)}, u32[]{:S(2)}) collective-permute-start(f32[1,1,68,256]{2,3,1,0:T(8,128)S(1)} %bitcast.24), channel_id=1, source_target_pairs={{2,0},{4,2},{6,4},{8,6},{10,8},{12,10},{14,12},{16,14},{18,16},{20... | collective-permute-start | bytes 208904 | tf_op jit(solution)/shard_map/ppermute | solution.py:29
  107.4 2.6 %collective-permute-done.4 = f32[1,1,68,256]{2,3,1,0:T(8,128)S(1)} collective-permute-done((f32[1,1,68,256]{2,3,1,0:T(8,128)S(1)}, f32[1,1,68,256]{2,3,1,0:T(8,128)S(1)}, u32[]{:S(2)}, u32[]{:S(2)}) %collective-permute-start.4) | collective-permute-done | bytes 69664 | tf_op jit(solution)/shard_map/ppermute | solution.py:28
  110.0 1.5 %collective-permute-start.6 = (f32[3,1,68,256]{2,3,1,0:T(8,128)S(1)}, f32[3,1,68,256]{2,3,1,0:T(8,128)S(1)}, u32[]{:S(2)}, u32[]{:S(2)}) collective-permute-start(f32[3,1,68,256]{2,3,1,0:T(8,128)S(1)} %pad_maximum_fusion.9), channel_id=1, source_target_pairs={{0,1},{1,0},{2,3},{3,2},{4,5},{5,4},{6,7},{7,6},{8,9},{9,8},{10,11... | collective-permute-start | bytes 626696 | tf_op jit(solution)/shard_map/ppermute | solution.py:28
  112.1 17.6 %fusion.27 = f32[3,2,8,64,128]{3,2,4,1,0:T(8,128)} fusion(f32[64,1,2,10,130]{0,3,4,2,1:T(8,128)} %get-tuple-element.16, f32[64,1,2,10,130]{0,3,4,2,1:T(8,128)} %get-tuple-element.17, f32[64,1,2,10,130]{0,3,4,2,1:T(8,128)} %get-tuple-element.18, f32[64,1,2,10,130]{0,3,4,2,1:T(8,128)} %get-tuple-element.19, f32[64,1,2,10,130]{0,3,4,2,1:T(8,128)S(1)} %get-tuple-element.15, ...), kind=kLoop, calls=%fused_computation.86 | loop fusion | flops 7077888 | bytes 11192320 | tf_op jit(solution)/shard_map/transpose | solution.py:336
  129.7 2.4 %copy.57 = f32[3,2,8,64,128]{4,3,2,1,0:T(8,128)S(1)} copy(f32[3,2,8,64,128]{3,2,4,1,0:T(8,128)} %fusion.27) | data formatting | bytes 3145728 | tf_op jit(solution)/shard_map/transpose | solution.py:336
  132.1 1.1 pad_maximum_fusion.8
  133.7 8.3 %shard_map.64 = f32[64,6,8,128]{3,2,1,0:T(8,128)} custom-call(f32[6,8,64,128]{3,2,1,0:T(8,128)S(1)} %bitcast.18, f32[9,64,256]{2,1,0:T(8,128)S(1)} %slice.192.table_ref, f32[9,4,256]{2,1,0:T(4,128)S(1)} %slice.193.extras_ref, s32[16,128]{1,0:T(8,128)S(1)} %bitcast.19, s32[16,1]{1,0:T(8,128)S(1)} %copy.67.count_ref), custom_call_target="tpu_custom_call" | custom-call | tf_op jit(solution)/shard_map/pallas_call | solution.py:298
  (44 shorter events, 5.0 us)
Async XLA Ops:
  0.0 9.6 %copy-start.5 = (s32[1,1,256]{2,1,0:T(1,128)S(1)}, s32[1,1,256]{2,1,0:T(1,128)}, u32[]{:S(2)}) copy-start(s32[1,1,256]{2,1,0:T(1,128)} %param.7) | copy-start | bytes 3076
  3.2 8.9 %copy-start.6 = (f32[1,1,256]{2,1,0:T(1,128)S(1)}, f32[1,1,256]{2,1,0:T(1,128)}, u32[]{:S(2)}) copy-start(f32[1,1,256]{2,1,0:T(1,128)} %param.8) | copy-start | bytes 3076
  3.2 13.5 %collective-permute-start = (f32[64,3,2,3,128]{4,0,3,2,1:T(8,128)}, f32[64,3,2,3,128]{4,0,3,2,1:T(8,128)}, u32[]{:S(2)}, u32[]{:S(2)}) collective-permute-start(f32[64,3,2,3,128]{4,0,3,2,1:T(8,128)} %copy.69), channel_id=1, source_target_pairs={{0,2},{2,4},{4,6},{6,8},{8,10},{10,12},{12,14},{14,16},{16,18},{18... | collective-permute-start | bytes 1769480 | tf_op jit(solution)/shard_map/ppermute | solution.py:28
  3.7 9.2 %copy-start.7 = (f32[1,1,256]{2,1,0:T(1,128)S(1)}, f32[1,1,256]{2,1,0:T(1,128)}, u32[]{:S(2)}) copy-start(f32[1,1,256]{2,1,0:T(1,128)} %param.9) | copy-start | bytes 3076
  4.6 14.5 %collective-permute-start.1 = (f32[64,3,2,3,128]{4,0,3,2,1:T(8,128)}, f32[64,3,2,3,128]{4,0,3,2,1:T(8,128)}, u32[]{:S(2)}, u32[]{:S(2)}) collective-permute-start(f32[64,3,2,3,128]{4,0,3,2,1:T(8,128)} %copy.70), channel_id=1, source_target_pairs={{2,0},{4,2},{6,4},{8,6},{10,8},{12,10},{14,12},{16,14},{18,16},{20... | collective-permute-start | bytes 1769480 | tf_op jit(solution)/shard_map/ppermute | solution.py:29
  21.4 8.9 %copy-start.3 = (f32[64,3,2,3,128]{0,3,4,2,1:T(4,128)S(1)}, f32[64,3,2,3,128]{0,3,4,2,1:T(4,128)}, u32[]{:S(2)}) copy-start(f32[64,3,2,3,128]{0,3,4,2,1:T(4,128)} %copy.54) | copy-start | bytes 1769476
  21.4 8.9 %copy-start.4 = (f32[64,3,2,3,128]{0,3,4,2,1:T(4,128)S(1)}, f32[64,3,2,3,128]{0,3,4,2,1:T(4,128)}, u32[]{:S(2)}) copy-start(f32[64,3,2,3,128]{0,3,4,2,1:T(4,128)} %copy.56) | copy-start | bytes 1769476
  22.5 5.2 %collective-permute-start.2 = (f32[64,3,2,14,3]{0,3,4,2,1:T(8,128)S(1)}, f32[64,3,2,14,3]{0,3,4,2,1:T(8,128)S(1)}, u32[]{:S(2)}, u32[]{:S(2)}) collective-permute-start(f32[64,3,2,14,3]{0,3,4,2,1:T(8,128)S(1)} %get-tuple-element.20), channel_id=1, source_target_pairs={{0,1},{1,0},{2,3},{3,2},{4,5},{5,4},{6,7},{7,6},{8,9},{9,8},{10,11... | collective-permute-start | bytes 193544 | tf_op jit(solution)/shard_map/ppermute | solution.py:28
  24.5 5.8 %collective-permute-start.3 = (f32[64,3,2,14,3]{0,3,4,2,1:T(8,128)S(1)}, f32[64,3,2,14,3]{0,3,4,2,1:T(8,128)S(1)}, u32[]{:S(2)}, u32[]{:S(2)}) collective-permute-start(f32[64,3,2,14,3]{0,3,4,2,1:T(8,128)S(1)} %get-tuple-element.21), channel_id=1, source_target_pairs={{1,0},{0,1},{3,2},{2,3},{5,4},{4,5},{7,6},{6,7},{9,8},{8,9},{11,10... | collective-permute-start | bytes 193544 | tf_op jit(solution)/shard_map/ppermute | solution.py:29
  51.8 3.1 %copy-start.1 = (f32[64,3,2,12,132]{0,3,4,2,1:T(8,128)}, f32[64,3,2,12,132]{0,3,4,2,1:T(8,128)S(1)}, u32[]{:S(2)}) copy-start(f32[64,3,2,12,132]{0,3,4,2,1:T(8,128)S(1)} %fusion.2) | copy-start | bytes 7299076
  81.7 7.0 %copy-start.2 = (f32[64,3,2,10,130]{0,3,4,2,1:T(8,128)S(1)}, f32[64,3,2,10,130]{0,3,4,2,1:T(8,128)}, u32[]{:S(2)}) copy-start(f32[64,3,2,10,130]{0,3,4,2,1:T(8,128)} %fusion.8) | copy-start | bytes 5990404
  99.0 8.4 %copy-start.8 = (s32[1,16]{1,0:T(1,128)S(1)}, s32[1,16]{1,0:T(1,128)}, u32[]{:S(2)}) copy-start(s32[1,16]{1,0:T(1,128)} %param.11) | copy-start | bytes 196
  102.9 7.1 %collective-permute-start.4 = (f32[1,1,68,256]{2,3,1,0:T(8,128)S(1)}, f32[1,1,68,256]{2,3,1,0:T(8,128)S(1)}, u32[]{:S(2)}, u32[]{:S(2)}) collective-permute-start(f32[1,1,68,256]{2,3,1,0:T(8,128)S(1)} %bitcast.23), channel_id=1, source_target_pairs={{0,2},{2,4},{4,6},{6,8},{8,10},{10,12},{12,14},{14,16},{16,18},{18... | collective-permute-start | bytes 208904 | tf_op jit(solution)/shard_map/ppermute | solution.py:28
  105.2 4.8 %collective-permute-start.5 = (f32[1,1,68,256]{2,3,1,0:T(8,128)S(1)}, f32[1,1,68,256]{2,3,1,0:T(8,128)S(1)}, u32[]{:S(2)}, u32[]{:S(2)}) collective-permute-start(f32[1,1,68,256]{2,3,1,0:T(8,128)S(1)} %bitcast.24), channel_id=1, source_target_pairs={{2,0},{4,2},{6,4},{8,6},{10,8},{12,10},{14,12},{16,14},{18,16},{20... | collective-permute-start | bytes 208904 | tf_op jit(solution)/shard_map/ppermute | solution.py:29
  110.0 22.1 %collective-permute-start.6 = (f32[3,1,68,256]{2,3,1,0:T(8,128)S(1)}, f32[3,1,68,256]{2,3,1,0:T(8,128)S(1)}, u32[]{:S(2)}, u32[]{:S(2)}) collective-permute-start(f32[3,1,68,256]{2,3,1,0:T(8,128)S(1)} %pad_maximum_fusion.9), channel_id=1, source_target_pairs={{0,1},{1,0},{2,3},{3,2},{4,5},{5,4},{6,7},{7,6},{8,9},{9,8},{10,11... | collective-permute-start | bytes 626696 | tf_op jit(solution)/shard_map/ppermute | solution.py:28
  111.5 20.6 %collective-permute-start.7 = (f32[3,1,68,256]{2,3,1,0:T(8,128)S(1)}, f32[3,1,68,256]{2,3,1,0:T(8,128)}, u32[]{:S(2)}, u32[]{:S(2)}) collective-permute-start(f32[3,1,68,256]{2,3,1,0:T(8,128)S(1)} %pad_maximum_fusion.9), channel_id=1, source_target_pairs={{1,0},{0,1},{3,2},{2,3},{5,4},{4,5},{7,6},{6,7},{9,8},{8,9},{11,10... | collective-permute-start | bytes 626696 | tf_op jit(solution)/shard_map/ppermute | solution.py:29
  132.1 1.6 %copy-start = (s32[1,16,128]{2,1,0:T(8,128)S(1)}, s32[1,16,128]{2,1,0:T(8,128)}, u32[]{:S(2)}) copy-start(s32[1,16,128]{2,1,0:T(8,128)} %param.10) | copy-start | bytes 24580

commit v2 on v1

--- a/solution.py
+++ b/solution.py
@@ -7,62 +7,12 @@
 from jax.experimental.pallas import tpu as pltpu
 from jax.sharding import PartitionSpec as P
 
-CX = 8
-CY = 128
 TILE_WIDTH_CELLS = 8
 STEPS = 3
 NS_ITERS = 3
 
 
 courant = 0.3
-highest = lax.Precision.HIGHEST
-
-
-def padded_2(x, sides, width):
-    for axis, dim in sides:
-        devices, length = (lax.axis_size(axis), x.shape[dim])
-        up = [(i, (i + 1) % devices) for i in range(devices)]
-        down = [(j, i) for i, j in up]
-        last = lax.slice_in_dim(x, length - width, length, axis=dim)
-        initial = lax.slice_in_dim(x, 0, width, axis=dim)
-        before = lax.ppermute(last, axis, up)
-        after = lax.ppermute(initial, axis, down)
-        x = jnp.concatenate([before, x, after], axis=dim)
-    return x
-
-
-def friedrichs_step(padded):
-    depths = 1.0 + padded[..., 0, :, :, :]
-    momentum_x = padded[..., 1, :, :, :]
-    momentum_y = padded[..., 2, :, :, :]
-    pressure = 0.5 * depths * depths
-    cross_flux = momentum_x * momentum_y / depths
-    flux_x = jnp.stack(
-        [momentum_x, momentum_x * momentum_x / depths + pressure, cross_flux], axis=-4
-    )
-    flux_y = jnp.stack(
-        [momentum_y, cross_flux, momentum_y * momentum_y / depths + pressure], axis=-4
-    )
-    neighbours = (
-        padded[..., 2:, 1:-1]
-        + padded[..., :-2, 1:-1]
-        + padded[..., 1:-1, 2:]
-        + padded[..., 1:-1, :-2]
-    )
-    return (
-        0.25 * neighbours
-        - 0.5 * courant * (flux_x[..., 2:, 1:-1] - flux_x[..., :-2, 1:-1])
-        - 0.5 * courant * (flux_y[..., 1:-1, 2:] - flux_y[..., 1:-1, :-2])
-    )
-
-
-def cut_outside(padded, patch_border):
-    extent = padded.shape[-1] - 2 * patch_border
-    global_rows = (
-        lax.iota(jnp.int32, padded.shape[-1]) + lax.axis_index("gy") * extent - patch_border
-    )
-    inside = (global_rows >= 0) & (global_rows < extent * lax.axis_size("gy"))
-    return padded * inside.astype(padded.dtype)
 
 
 def split(x):
@@ -76,6 +26,295 @@
 
 def dot_nt(a, b):
     return lax.dot_general(a, b, (((1,), (1,)), ((), ())), preferred_element_type=jnp.float32)
+
+
+NEIGHBOURS = [(x, y) for x in (-1, 0, 1) for y in (-1, 0, 1) if (x, y) != (0, 0)]
+CHUNKS = 4
+
+
+def fluxes(q):
+    depth, east, north = q
+    height = 1.0 + depth
+    inverse = 1.0 / height
+    pressure = 0.5 * height * height
+    speed = east * inverse
+    cross = speed * north
+    flux_x = (east, east * speed + pressure, cross)
+    flux_y = (north, cross, north * north * inverse + pressure)
+    quarter = [0.25 * v for v in q]
+    flux_x = [0.5 * courant * f for f in flux_x]
+    flux_y = [0.5 * courant * f for f in flux_y]
+    return (
+        [v - f for v, f in zip(quarter, flux_x)],
+        [v + f for v, f in zip(quarter, flux_x)],
+        [v - f for v, f in zip(quarter, flux_y)],
+        [v + f for v, f in zip(quarter, flux_y)],
+    )
+
+
+def forecast_kernel(
+    rows_in_x, rows_in_y, prior_ref, column_ref, value_ref, precision_ref,
+    state_ref, table_out, extras_out,
+    main, strips, north_strips, south_strips, inserts, table, extras,
+    load_sem, halo_send, halo_recv, strip_send, strip_recv, obs_send, obs_recv,
+    extra_send, extra_recv,
+):
+    members, kinds, columns, lanes = prior_ref.shape
+    levels = kinds // 3
+    slots = column_ref.shape[1]
+    pad = STEPS
+    wide = columns + 2 * pad
+    me_x, me_y = lax.axis_index("gx"), lax.axis_index("gy")
+
+    def there(dx, dy):
+        return {"gx": lax.rem(me_x + dx + rows_in_x, rows_in_x), "gy": me_y + dy}
+
+    def exists(dy):
+        return (me_y + dy >= 0) & (me_y + dy < rows_in_y)
+
+    def each(act):
+        for dx, dy in NEIGHBOURS:
+            if dy == 0:
+                act(dx, dy)
+            else:
+                pl.when(exists(dy))(functools.partial(act, dx, dy))
+
+    loads = []
+    for column in [*range(columns - pad, columns), *range(columns - pad)]:
+        for kind in range(kinds):
+            loads.append(
+                pltpu.make_async_copy(
+                    prior_ref.at[:, kind, column, :], main.at[kind, pad + column],
+                    load_sem.at[kind, column],
+                )
+            )
+            loads[-1].start()
+
+    barrier = pltpu.get_barrier_semaphore()
+
+    def greet(dx, dy):
+        pl.semaphore_signal(barrier, 1, device_id=there(dx, dy))
+
+    each(greet)
+    sides = exists(-1).astype(jnp.int32) + exists(1).astype(jnp.int32)
+    pl.semaphore_wait(barrier, 2 + 3 * sides)
+
+    for load in loads:
+        load.wait()
+
+    def span(chunk):
+        size = members // CHUNKS
+        return pl.ds(chunk * size, size)
+
+    def halo(side, chunk):
+        start, stop = (columns, 0) if side == 0 else (pad, pad + columns)
+        return pltpu.make_async_remote_copy(
+            main.at[:, pl.ds(start, pad), span(chunk), :],
+            main.at[:, pl.ds(stop, pad), span(chunk), :],
+            halo_send.at[side, chunk], halo_recv.at[side, chunk],
+            device_id=there(1 - 2 * side, 0),
+        )
+
+    def mirrored(dx, dy):
+        return (1 - dx) * 3 + 1 - dy
+
+    def seen(dx, dy):
+        return (1 + dx) * 3 + 1 + dy
+
+    def strip_copy(dx, dy, source):
+        start = {1: columns, 0: pad, -1: pad}[dx]
+        stop = {1: 0, 0: pad, -1: pad + columns}[dx]
+        count = columns if dx == 0 else pad
+        target = {1: south_strips, 0: strips, -1: north_strips}[dy]
+        return pltpu.make_async_remote_copy(
+            strips.at[:, pl.ds(start, count)], target.at[:, pl.ds(stop, count)],
+            strip_send.at[seen(dx, dy)], strip_recv.at[mirrored(dx, dy)],
+            device_id=source,
+        )
+
+    def table_copy(ref, send, recv, dx, dy, device):
+        return pltpu.make_async_remote_copy(
+            ref.at[4], ref.at[mirrored(dx, dy)],
+            send.at[seen(dx, dy)], recv.at[mirrored(dx, dy)], device_id=device,
+        )
+
+    for side in range(2):
+        halo(side, 0).start()
+
+    lane = lax.broadcasted_iota(jnp.int32, (8, lanes), 1)
+    groups = members // 8
+    width = lanes // groups
+    half = width // 4
+    group_lane = lane % width
+
+    def pack(index, carry):
+        kind, column = index // columns, index % columns
+        row = main[kind, pad + column]
+        packed = jnp.zeros((8, lanes), jnp.float32)
+        for group in range(groups):
+            part = row[8 * group : 8 * group + 8]
+            base = group * width
+            upper = pltpu.roll(part, (base + half) % lanes, 1)
+            lower = pltpu.roll(part, (base + 3 * half) % lanes, 1)
+            packed = jnp.where((lane >= base) & (lane < base + half), upper, packed)
+            packed = jnp.where((lane >= base + 3 * half) & (lane < base + width), lower, packed)
+        strips[kind, pad + column] = packed
+        return carry
+
+    lax.fori_loop(0, kinds * columns, pack, 0)
+    each(lambda dx, dy: strip_copy(dx, dy, there(dx, dy)).start())
+
+    where = column_ref[...]
+    extras[4, 0:1, :] = value_ref[...]
+    extras[4, 1:2, :] = precision_ref[...]
+    extras[4, 2:3, :] = lax.div(where, lanes).astype(jnp.float32)
+    extras[4, 3:4, :] = lax.rem(where, lanes).astype(jnp.float32)
+    extras[4, 4:8, :] = jnp.zeros((4, slots), jnp.float32)
+    each(lambda dx, dy: table_copy(extras, extra_send, extra_recv, dx, dy, there(dx, dy)).start())
+    for chunk in range(1, CHUNKS):
+        for side in range(2):
+            halo(side, chunk).start()
+
+    each(lambda dx, dy: strip_copy(-dx, -dy, there(dx, dy)).wait_recv())
+
+    has_north = jnp.where(exists(1), 1.0, 0.0)
+    has_south = jnp.where(exists(-1), 1.0, 0.0)
+    own = (group_lane < half) | (group_lane >= 3 * half)
+    northern = group_lane < 2 * half
+
+    def inside(v):
+        kept = jnp.where(northern, has_north, has_south) > 0.5
+        return jnp.where((own | kept)[None], v, 0.0)
+
+    for level in range(levels):
+        q = []
+        for field in range(3):
+            kind = field * levels + level
+            beyond = jnp.where(
+                northern[None],
+                pltpu.roll(north_strips[kind], lanes - 2 * half, 2),
+                pltpu.roll(south_strips[kind], 2 * half, 2),
+            )
+            q.append(inside(jnp.where(own[None], strips[kind], beyond)))
+        for step in range(STEPS):
+            east, west, north, south = fluxes(q)
+            rows = q[0].shape[0]
+            fresh = []
+            for field in range(3):
+                up, down = north[field][1 : rows - 1], south[field][1 : rows - 1]
+                inserts[step, field * levels + level, 0 : rows - 2] = jnp.where(
+                    (group_lane == half)[None], up, pltpu.roll(down, lanes - 2 * half + 2, 2)
+                )
+                fresh.append(
+                    inside(
+                        east[field][2:]
+                        + west[field][: rows - 2]
+                        + pltpu.roll(up, lanes - 1, 2)
+                        + pltpu.roll(down, 1, 2)
+                    )
+                )
+            q = fresh
+
+    def advance(index, carry):
+        group, level = index // levels, index % levels
+        part = pl.ds(pl.multiple_of(group * 8, 8), 8)
+        turn = lax.rem(2 * lanes - 1 - half - group * width, lanes)
+        q = [main[field * levels + level, :, part, :] for field in range(3)]
+        for step in range(STEPS):
+            east, west, north, south = fluxes(q)
+            rows = q[0].shape[0]
+            fresh = []
+            for field in range(3):
+                edge = pltpu.roll(inserts[step, field * levels + level, 0 : rows - 2], turn, 2)
+                up = pltpu.roll(north[field][1 : rows - 1], lanes - 1, 2)
+                down = pltpu.roll(south[field][1 : rows - 1], 1, 2)
+                fresh.append(
+                    east[field][2:]
+                    + west[field][: rows - 2]
+                    + jnp.where((lane == lanes - 1)[None], edge, up)
+                    + jnp.where((lane == 0)[None], edge, down)
+                )
+            q = fresh
+        for field in range(3):
+            state_ref[field * levels + level, :, part, :] = q[field]
+        return carry
+
+    per_chunk = groups // CHUNKS * levels
+    for chunk in range(CHUNKS):
+        for side in range(2):
+            halo(side, chunk).wait_recv()
+        lax.fori_loop(chunk * per_chunk, (chunk + 1) * per_chunk, advance, 0)
+
+    cell = lax.broadcasted_iota(jnp.int32, (lanes, slots), 0)
+    observed = jnp.zeros((3 * members, slots), jnp.float32)
+    for column in range(columns):
+        layers = state_ref[0, column]
+        for level in range(1, levels):
+            layers = layers + state_ref[level, column]
+        layers = layers / levels
+        first, rest = split(layers)
+        second = layers - first.astype(jnp.float32) - rest.astype(jnp.float32)
+        stacked = jnp.concatenate([first, rest, second.astype(jnp.bfloat16)], axis=0)
+        chosen = (cell + column * lanes == where).astype(jnp.float32).astype(jnp.bfloat16)
+        observed += dot_nn(stacked, chosen)
+    table[4] = observed[:members] + observed[members : 2 * members] + observed[2 * members :]
+    each(lambda dx, dy: table_copy(table, obs_send, obs_recv, dx, dy, there(dx, dy)).start())
+
+    table_out[4] = table[4]
+    extras_out[4] = extras[4]
+
+    def receive(dx, dy):
+        for ref, send, recv, out in (
+            (extras, extra_send, extra_recv, extras_out),
+            (table, obs_send, obs_recv, table_out),
+        ):
+            table_copy(ref, send, recv, -dx, -dy, there(dx, dy)).wait_recv()
+            out[seen(dx, dy)] = ref[seen(dx, dy)]
+
+    each(receive)
+    for chunk in range(CHUNKS):
+        for side in range(2):
+            halo(side, chunk).wait_send()
+
+    def sent(dx, dy):
+        strip_copy(dx, dy, there(dx, dy)).wait_send()
+        table_copy(extras, extra_send, extra_recv, dx, dy, there(dx, dy)).wait_send()
+        table_copy(table, obs_send, obs_recv, dx, dy, there(dx, dy)).wait_send()
+
+    each(sent)
+
+
+def forecast(prior, obs_column, obs_value, obs_precision):
+    members, kinds, columns, lanes = prior.shape
+    slots = obs_column.shape[1]
+    wide = columns + 2 * STEPS
+    vmem = pl.BlockSpec(memory_space=pltpu.VMEM)
+    return pl.pallas_call(
+        functools.partial(forecast_kernel, lax.axis_size("gx"), lax.axis_size("gy")),
+        out_shape=(
+            jax.ShapeDtypeStruct((kinds, columns, members, lanes), jnp.float32),
+            jax.ShapeDtypeStruct((9, members, slots), jnp.float32),
+            jax.ShapeDtypeStruct((9, 8, slots), jnp.float32),
+        ),
+        in_specs=[pl.BlockSpec(memory_space=pl.ANY), vmem, vmem, vmem],
+        out_specs=(vmem, vmem, vmem),
+        scratch_shapes=[
+            pltpu.VMEM((kinds, wide, members, lanes), jnp.float32),
+            pltpu.VMEM((kinds, wide, 8, lanes), jnp.float32),
+            pltpu.VMEM((kinds, wide, 8, lanes), jnp.float32),
+            pltpu.VMEM((kinds, wide, 8, lanes), jnp.float32),
+            pltpu.VMEM((STEPS, kinds, wide, 8, lanes), jnp.float32),
+            pltpu.VMEM((9, members, slots), jnp.float32),
+            pltpu.VMEM((9, 8, slots), jnp.float32),
+            pltpu.SemaphoreType.DMA((kinds, columns)),
+            pltpu.SemaphoreType.DMA((2, CHUNKS)),
+            pltpu.SemaphoreType.DMA((2, CHUNKS)),
+        ]
+        + [pltpu.SemaphoreType.DMA((9,))] * 6,
+        compiler_params=pltpu.CompilerParams(
+            collective_id=0, has_side_effects=True, vmem_limit_bytes=24 << 20
+        ),
+    )(prior, obs_column, obs_value, obs_precision)
 
 
 def analysis_kernel(
@@ -309,44 +548,27 @@
             pltpu.VMEM(fields.shape, jnp.float32),
             pltpu.SemaphoreType.DMA((kinds * columns,)),
         ],
-        compiler_params=pltpu.CompilerParams(vmem_limit_bytes=40 << 20),
+        compiler_params=pltpu.CompilerParams(vmem_limit_bytes=24 << 20),
     )(fields, table, extras, entries, counts)
 
 
 def local(prior_members, obs_column, obs_value, obs_precision, obs_list, patch_count):
-    members = prior_members.shape[0]
-    levels = prior_members.shape[2]
-    width_x = prior_members.shape[3]
-    width_y = prior_members.shape[4]
-    states = prior_members
-    padded = padded_2(states, (("gx", 3), ("gy", 4)), STEPS)
-    for repeat in range(STEPS):
-        padded = friedrichs_step(cut_outside(padded, STEPS - repeat))
-    states = padded
-    layer_mean_value = jnp.mean(states[:, 0], axis=1).reshape(members, width_x * width_y)
-    columns = obs_column[0, 0]
-    members_obs = jnp.take(layer_mean_value, columns, axis=1)
-    local_x = (columns // width_y).astype(jnp.float32)
-    local_y = (columns % width_y).astype(jnp.float32)
-    extras = jnp.stack([obs_value[0, 0], obs_precision[0, 0], local_x, local_y], axis=0)
-    obs_info = jnp.concatenate([members_obs, extras], axis=0)[None, None]
-    beside_all = padded_2(obs_info, (("gx", 0), ("gy", 1)), 1)
-    info_rows, slot_total = beside_all.shape[2:]
-    everything = beside_all.reshape(9, info_rows, slot_total)
-    fields = jnp.transpose(states, (1, 2, 3, 0, 4)).reshape(
-        3 * levels, width_x, members, width_y
+    members, fields, levels, width_x, width_y = prior_members.shape
+    state, table, extras = forecast(
+        prior_members.reshape(members, fields * levels, width_x, width_y),
+        obs_column[0], obs_value[0], obs_precision[0],
     )
     batch = obs_list.shape[0] * obs_list.shape[1]
     result = analyse(
-        fields,
-        everything[:, :members],
-        everything[:, members:],
+        state,
+        table,
+        extras,
         obs_list.reshape(batch, obs_list.shape[2]),
         patch_count.reshape(batch, 1),
         width_x,
         width_y,
     )
-    return result.reshape(members, 3, levels, width_x, width_y)
+    return result.reshape(prior_members.shape)
 
 
 def solution(mesh):

time: 143 us -> 48.4 us (0.34)
  other arithmetic: 88 us -> 0 us
  Pallas kernels: 8.33 us -> 43.8 us
  local copies, waits for them, and re-layouts: 20.2 us -> 4.19 us
  starting transfers between devices: 14.2 us -> 0 us
  waiting for transfers between devices: 11.1 us -> 0 us
    mul x3 -> x0, other arithmetic: 36.8 us -> none  [cut_outside(): return padded * inside.astype(padded.dtype)]
    pallas_call x0 -> x1, Pallas kernels: none -> 35.5 us  [forecast(): pl.pallas_call(functools.partial(forecast_kernel, lax.axis_size('gx'), la...]
    transpose x1 -> x0, other arithmetic: 17.6 us -> none  [local(): jnp.transpose(states, (1, 2, 3, 0, 4))]
    ppermute x8 -> x0, starting transfers between devices: 14.2 us -> none  [the longest x4 7.8 us: padded_2(): after = lax.ppermute(initial, axis, down)]
    ppermute x8 -> x0, waiting for transfers between devices: 11.1 us -> none  [the longest x4 8.5 us: padded_2(): before = lax.ppermute(last, axis, up)]
    another operation x2 -> x0, other arithmetic: 10.6 us -> none  [friedrichs_step(): jnp.stack([momentum_x, momentum_x * momentum_x / depths + pressure, cross...]
    sub x1 -> x0, other arithmetic: 10.3 us -> none  [friedrichs_step(): 0.25 * neighbours]
    slice x4 -> x0, other arithmetic: 10 us -> none  [the longest x3 8.97 us: friedrichs_step(): momentum_x = padded[..., 1, :, :, :]]
  transfers between devices with their start and end apart: 8 -> 0, of which waited for: 4 -> 0; matrix products, arithmetic and copies ran while one was open for 19% -> 0% of each run, Pallas kernels for 0% -> 0%
where the time goes in v2:
time: 48.4 us; the launch traced here: 48.2 us
  Pallas kernels  43.8 us (90%)
  local copies, waits for them, and re-layouts  4.19 us (9%)
    pallas_call x1, Pallas kernels, forecast(): pl.pallas_call(functools.partial(forecast_kernel, lax.axis_size('gx'), la...  35.5 us
    pallas_call x1, Pallas kernels, analyse(): pl.pallas_call(functools.partial(analysis_kernel, geometry), out_shape=ja...  8.3 us
    unnamed x10, local copies, waits for them, and re-layouts  3.45 us

profile of v2, /device:TPU:0, one launch (start us, length us, event | category | flops | bytes accessed | tf_op | source)
XLA Modules:
  0.0 48.2 jit_solution(1731014415745955076)
XLA Ops:
  0.0 0.0 copy-start.1
  0.0 0.7 %copy.7.count_ref = s32[16,1]{1,0:T(8,128)S(1)} copy(s32[16,1]{0,1:T(1,128)} %bitcast.12) | data formatting | bytes 128 | tf_op jit(solution)/shard_map/reshape | solution.py:567
  0.7 0.0 copy-start
  0.8 1.4 %copy-done = f32[64,3,2,8,128]{4,3,2,1,0:T(8,128)S(1)} copy-done((f32[64,3,2,8,128]{4,3,2,1,0:T(8,128)S(1)}, f32[64,3,2,8,128]{4,3,2,1,0:T(8,128)}, u32[]{:S(2)}) %copy-start) | copy-done | bytes 1572888
  2.2 0.0 copy-start.2
  2.2 0.7 %copy-done.2 = s32[1,1,256]{2,1,0:T(1,128)S(1)} copy-done((s32[1,1,256]{2,1,0:T(1,128)S(1)}, s32[1,1,256]{2,1,0:T(1,128)}, u32[]{:S(2)}) %copy-start.2) | copy-done | bytes 1048
  2.8 0.0 copy-start.3
  2.8 0.7 %copy-done.3 = f32[1,1,256]{2,1,0:T(1,128)S(1)} copy-done((f32[1,1,256]{2,1,0:T(1,128)S(1)}, f32[1,1,256]{2,1,0:T(1,128)}, u32[]{:S(2)}) %copy-start.3) | copy-done | bytes 1048
  3.5 0.0 copy-start.4
  3.5 0.7 %copy-done.4 = f32[1,1,256]{2,1,0:T(1,128)S(1)} copy-done((f32[1,1,256]{2,1,0:T(1,128)S(1)}, f32[1,1,256]{2,1,0:T(1,128)}, u32[]{:S(2)}) %copy-start.4) | copy-done | bytes 1048
  4.2 35.5 %shard_map.64 = (f32[6,8,64,128]{3,2,1,0:T(8,128)S(1)}, f32[9,64,256]{2,1,0:T(8,128)S(1)}, f32[9,8,256]{2,1,0:T(8,128)S(1)}) custom-call(f32[64,6,8,128]{3,2,1,0:T(8,128)S(1)} %bitcast.7, s32[1,256]{1,0:T(1,128)S(1)} %bitcast.9, f32[1,256]{1,0:T(1,128)S(1)} %bitcast.10, f32[1,256]{1,0:T(1,128)S(1)} %bitcast.11), custom_call_target="tpu_custom_call" | custom-call | tf_op jit(solution)/shard_map/pallas_call | solution.py:292
  39.7 0.0 copy-done.1
  39.7 8.3 %shard_map.65 = f32[64,6,8,128]{3,2,1,0:T(8,128)} custom-call(f32[6,8,64,128]{3,2,1,0:T(8,128)S(1)} %get-tuple-element.8.fields_ref, f32[9,64,256]{2,1,0:T(8,128)S(1)} %get-tuple-element.9.table_ref, f32[9,8,256]{2,1,0:T(8,128)S(1)} %get-tuple-element.10.extras_ref, s32[16,128]{1,0:T(8,128)S(1)} %bitcast.8, s32[16,1]{1,0:T(8,128)S(1)} %copy.7.count_ref), custom_call_target="tpu_custom_call" | custom-call | tf_op jit(solution)/shard_map/pallas_call | solution.py:537
Async XLA Ops:
  0.0 39.7 %copy-start.1 = (s32[1,16,128]{2,1,0:T(8,128)S(1)}, s32[1,16,128]{2,1,0:T(8,128)}, u32[]{:S(2)}) copy-start(s32[1,16,128]{2,1,0:T(8,128)} %param.10) | copy-start | bytes 24580
  0.7 1.4 %copy-start = (f32[64,3,2,8,128]{4,3,2,1,0:T(8,128)S(1)}, f32[64,3,2,8,128]{4,3,2,1,0:T(8,128)}, u32[]{:S(2)}) copy-start(f32[64,3,2,8,128]{4,3,2,1,0:T(8,128)} %param.6) | copy-start | bytes 4718596
  2.2 0.7 %copy-start.2 = (s32[1,1,256]{2,1,0:T(1,128)S(1)}, s32[1,1,256]{2,1,0:T(1,128)}, u32[]{:S(2)}) copy-start(s32[1,1,256]{2,1,0:T(1,128)} %param.7) | copy-start | bytes 3076
  2.8 0.7 %copy-start.3 = (f32[1,1,256]{2,1,0:T(1,128)S(1)}, f32[1,1,256]{2,1,0:T(1,128)}, u32[]{:S(2)}) copy-start(f32[1,1,256]{2,1,0:T(1,128)} %param.8) | copy-start | bytes 3076
  3.5 0.7 %copy-start.4 = (f32[1,1,256]{2,1,0:T(1,128)S(1)}, f32[1,1,256]{2,1,0:T(1,128)}, u32[]{:S(2)}) copy-start(f32[1,1,256]{2,1,0:T(1,128)} %param.9) | copy-start | bytes 3076

commit v3 on v2

--- a/solution.py
+++ b/solution.py
@@ -55,8 +55,8 @@
 def forecast_kernel(
     rows_in_x, rows_in_y, prior_ref, column_ref, value_ref, precision_ref,
     state_ref, table_out, extras_out,
-    main, strips, north_strips, south_strips, inserts, table, extras,
-    load_sem, halo_send, halo_recv, strip_send, strip_recv, obs_send, obs_recv,
+    main, strips, dense_north, dense_south, north_strips, south_strips, inserts, table,
+    extras, column_vmem, info_sem, load_sem, halo_send, halo_recv, strip_send, strip_recv, obs_send, obs_recv,
     extra_send, extra_recv,
 ):
     members, kinds, columns, lanes = prior_ref.shape
@@ -89,6 +89,15 @@
                 )
             )
             loads[-1].start()
+    for index, (source, target) in enumerate(
+        (
+            (column_ref, column_vmem),
+            (value_ref, extras.at[4, 0:1]),
+            (precision_ref, extras.at[4, 1:2]),
+        )
+    ):
+        loads.append(pltpu.make_async_copy(source, target, info_sem.at[index]))
+        loads[-1].start()
 
     barrier = pltpu.get_barrier_semaphore()
 
@@ -121,15 +130,17 @@
     def seen(dx, dy):
         return (1 + dx) * 3 + 1 + dy
 
-    def strip_copy(dx, dy, source):
+    def strip_copy(dx, dy, device):
         start = {1: columns, 0: pad, -1: pad}[dx]
         stop = {1: 0, 0: pad, -1: pad + columns}[dx]
         count = columns if dx == 0 else pad
         target = {1: south_strips, 0: strips, -1: north_strips}[dy]
+        source = {1: dense_north, 0: strips, -1: dense_south}[dy]
+        start = start if dy == 0 else start - pad
         return pltpu.make_async_remote_copy(
-            strips.at[:, pl.ds(start, count)], target.at[:, pl.ds(stop, count)],
+            source.at[:, pl.ds(start, count)], target.at[:, pl.ds(stop, count)],
             strip_send.at[seen(dx, dy)], strip_recv.at[mirrored(dx, dy)],
-            device_id=source,
+            device_id=device,
         )
 
     def table_copy(ref, send, recv, dx, dy, device):
@@ -147,26 +158,33 @@
     half = width // 4
     group_lane = lane % width
 
-    def pack(index, carry):
-        kind, column = index // columns, index % columns
-        row = main[kind, pad + column]
-        packed = jnp.zeros((8, lanes), jnp.float32)
+    def pack(kind, carry):
+        raw = jnp.zeros((columns, 8, lanes), jnp.float32)
         for group in range(groups):
-            part = row[8 * group : 8 * group + 8]
+            part = main[kind, pad : pad + columns, 8 * group : 8 * group + 8, :]
             base = group * width
-            upper = pltpu.roll(part, (base + half) % lanes, 1)
-            lower = pltpu.roll(part, (base + 3 * half) % lanes, 1)
-            packed = jnp.where((lane >= base) & (lane < base + half), upper, packed)
-            packed = jnp.where((lane >= base + 3 * half) & (lane < base + width), lower, packed)
-        strips[kind, pad + column] = packed
+            moved = pltpu.roll(part, base + half, 2)
+            raw = jnp.where(((lane >= base) & (lane < base + width))[None], moved, raw)
+        strips[kind, pad : pad + columns] = jnp.where(
+            (group_lane < half)[None], raw, pltpu.roll(raw, 2 * half, 2)
+        )
         return carry
 
-    lax.fori_loop(0, kinds * columns, pack, 0)
+    lax.fori_loop(0, kinds, pack, 0)
+    for level in range(levels):
+        for dense, place in ((dense_north, 0), (dense_south, 3)):
+            tile = None
+            for field in range(3):
+                piece = strips[field * levels + level, pad : pad + columns]
+                shift = (field - place) * half % lanes
+                piece = pltpu.roll(piece, shift, 2) if shift else piece
+                tile = piece if field == 0 else jnp.where(
+                    (group_lane // half == field)[None], piece, tile
+                )
+            dense[level] = tile
     each(lambda dx, dy: strip_copy(dx, dy, there(dx, dy)).start())
 
-    where = column_ref[...]
-    extras[4, 0:1, :] = value_ref[...]
-    extras[4, 1:2, :] = precision_ref[...]
+    where = column_vmem[...]
     extras[4, 2:3, :] = lax.div(where, lanes).astype(jnp.float32)
     extras[4, 3:4, :] = lax.rem(where, lanes).astype(jnp.float32)
     extras[4, 4:8, :] = jnp.zeros((4, slots), jnp.float32)
@@ -192,8 +210,8 @@
             kind = field * levels + level
             beyond = jnp.where(
                 northern[None],
-                pltpu.roll(north_strips[kind], lanes - 2 * half, 2),
-                pltpu.roll(south_strips[kind], 2 * half, 2),
+                pltpu.roll(north_strips[level], (1 - field) * half % lanes, 2),
+                pltpu.roll(south_strips[level], (2 - field) * half % lanes, 2),
             )
             q.append(inside(jnp.where(own[None], strips[kind], beyond)))
         for step in range(STEPS):
@@ -296,16 +314,20 @@
             jax.ShapeDtypeStruct((9, members, slots), jnp.float32),
             jax.ShapeDtypeStruct((9, 8, slots), jnp.float32),
         ),
-        in_specs=[pl.BlockSpec(memory_space=pl.ANY), vmem, vmem, vmem],
+        in_specs=[pl.BlockSpec(memory_space=pltpu.HBM)] * 4,
         out_specs=(vmem, vmem, vmem),
         scratch_shapes=[
             pltpu.VMEM((kinds, wide, members, lanes), jnp.float32),
             pltpu.VMEM((kinds, wide, 8, lanes), jnp.float32),
-            pltpu.VMEM((kinds, wide, 8, lanes), jnp.float32),
-            pltpu.VMEM((kinds, wide, 8, lanes), jnp.float32),
+            pltpu.VMEM((kinds // 3, columns, 8, lanes), jnp.float32),
+            pltpu.VMEM((kinds // 3, columns, 8, lanes), jnp.float32),
+            pltpu.VMEM((kinds // 3, wide, 8, lanes), jnp.float32),
+            pltpu.VMEM((kinds // 3, wide, 8, lanes), jnp.float32),
             pltpu.VMEM((STEPS, kinds, wide, 8, lanes), jnp.float32),
             pltpu.VMEM((9, members, slots), jnp.float32),
             pltpu.VMEM((9, 8, slots), jnp.float32),
+            pltpu.VMEM((1, slots), jnp.int32),
+            pltpu.SemaphoreType.DMA((3,)),
             pltpu.SemaphoreType.DMA((kinds, columns)),
             pltpu.SemaphoreType.DMA((2, CHUNKS)),
             pltpu.SemaphoreType.DMA((2, CHUNKS)),
@@ -335,7 +357,7 @@
     lane_id = lax.broadcasted_iota(jnp.int32, (128, capacity), 0)
     for patch in range(batch):
         named = list_ref[patch : patch + 1, :]
-        usable = usable_at < count_ref[patch : patch + 1, :]
+        usable = usable_at < count_ref[patch // patches_y, patch % patches_y]
         upper = jnp.where(usable, named // 128, -1)
         lower = named % 128
         counts = dot_nt(
@@ -537,7 +559,7 @@
     return pl.pallas_call(
         functools.partial(analysis_kernel, geometry),
         out_shape=jax.ShapeDtypeStruct((members, kinds, columns, lanes), jnp.float32),
-        in_specs=[vmem] * 5,
+        in_specs=[vmem] * 4 + [pl.BlockSpec(memory_space=pltpu.SMEM)],
         out_specs=pl.BlockSpec(memory_space=pl.ANY),
         scratch_shapes=[
             pltpu.VMEM((tiles, batch, slots), jnp.float32),
@@ -564,7 +586,7 @@
         table,
         extras,
         obs_list.reshape(batch, obs_list.shape[2]),
-        patch_count.reshape(batch, 1),
+        patch_count,
         width_x,
         width_y,
     )

time: 48.4 us -> 43.5 us (0.90)
  the two profiles are of different devices: /device:TPU:0 before, /device:TPU:1 now
where the time goes in v3:
time: 43.5 us; the launch traced here: 43.3 us
  Pallas kernels  39.6 us (91%)
  local copies, waits for them, and re-layouts  3.47 us (8%)
    pallas_call x1, Pallas kernels, forecast(): pl.pallas_call(functools.partial(forecast_kernel, lax.axis_size('gx'), la...  30.8 us
    pallas_call x1, Pallas kernels, analyse(): pl.pallas_call(functools.partial(analysis_kernel, geometry), out_shape=ja...  8.83 us
    unnamed x12, local copies, waits for them, and re-layouts  3.47 us

profile of v3, /device:TPU:1, one launch (start us, length us, event | category | flops | bytes accessed | tf_op | source)
XLA Modules:
  0.0 43.3 jit_solution(11319370764658941116)
XLA Ops:
  0.0 0.0 copy-start.5
  0.0 0.0 copy-start.1
  0.0 0.0 copy-start
  0.0 1.4 %copy-done = f32[64,3,2,8,128]{4,3,2,1,0:T(8,128)S(1)} copy-done((f32[64,3,2,8,128]{4,3,2,1,0:T(8,128)S(1)}, f32[64,3,2,8,128]{4,3,2,1,0:T(8,128)}, u32[]{:S(2)}) %copy-start) | copy-done | bytes 1572888
  1.4 0.0 copy-start.2
  1.4 0.7 %copy-done.2 = s32[1,1,256]{2,1,0:T(1,128)S(1)} copy-done((s32[1,1,256]{2,1,0:T(1,128)S(1)}, s32[1,1,256]{2,1,0:T(1,128)}, u32[]{:S(2)}) %copy-start.2) | copy-done | bytes 1048
  2.1 0.0 copy-start.3
  2.1 0.7 %copy-done.3 = f32[1,1,256]{2,1,0:T(1,128)S(1)} copy-done((f32[1,1,256]{2,1,0:T(1,128)S(1)}, f32[1,1,256]{2,1,0:T(1,128)}, u32[]{:S(2)}) %copy-start.3) | copy-done | bytes 1048
  2.8 0.0 copy-start.4
  2.8 0.7 %copy-done.4 = f32[1,1,256]{2,1,0:T(1,128)S(1)} copy-done((f32[1,1,256]{2,1,0:T(1,128)S(1)}, f32[1,1,256]{2,1,0:T(1,128)}, u32[]{:S(2)}) %copy-start.4) | copy-done | bytes 1048
  3.5 30.8 %shard_map.64 = (f32[6,8,64,128]{3,2,1,0:T(8,128)S(1)}, f32[9,64,256]{2,1,0:T(8,128)S(1)}, f32[9,8,256]{2,1,0:T(8,128)S(1)}) custom-call(f32[64,6,8,128]{3,2,1,0:T(8,128)S(1)} %bitcast.6, s32[1,256]{1,0:T(1,128)S(1)} %bitcast.8, f32[1,256]{1,0:T(1,128)S(1)} %bitcast.9, f32[1,256]{1,0:T(1,128)S(1)} %bitcast.10), custom_call_target="tpu_custom_call" | custom-call | tf_op jit(solution)/shard_map/pallas_call | solution.py:310
  34.3 0.0 copy-done.5
  34.3 0.0 copy-done.1
  34.3 8.8 %shard_map.65 = f32[64,6,8,128]{3,2,1,0:T(8,128)} custom-call(f32[6,8,64,128]{3,2,1,0:T(8,128)S(1)} %get-tuple-element.8.fields_ref, f32[9,64,256]{2,1,0:T(8,128)S(1)} %get-tuple-element.9.table_ref, f32[9,8,256]{2,1,0:T(8,128)S(1)} %get-tuple-element.10.extras_ref, s32[16,128]{1,0:T(8,128)S(1)} %bitcast.7, s32[1,16]{1,0:T(1,128)S(1)} %copy-done.5), custom_call_target="tpu_custom_call" | custom-call | tf_op jit(solution)/shard_map/pallas_call | solution.py:559
Async XLA Ops:
  0.0 34.3 %copy-start.5 = (s32[1,16]{1,0:T(1,128)S(1)}, s32[1,16]{1,0:T(1,128)}, u32[]{:S(2)}) copy-start(s32[1,16]{1,0:T(1,128)} %count_ref.1) | copy-start | bytes 196
  0.0 34.3 %copy-start.1 = (s32[1,16,128]{2,1,0:T(8,128)S(1)}, s32[1,16,128]{2,1,0:T(8,128)}, u32[]{:S(2)}) copy-start(s32[1,16,128]{2,1,0:T(8,128)} %param.10) | copy-start | bytes 24580
  0.0 1.4 %copy-start = (f32[64,3,2,8,128]{4,3,2,1,0:T(8,128)S(1)}, f32[64,3,2,8,128]{4,3,2,1,0:T(8,128)}, u32[]{:S(2)}) copy-start(f32[64,3,2,8,128]{4,3,2,1,0:T(8,128)} %param.6) | copy-start | bytes 4718596
  1.4 0.7 %copy-start.2 = (s32[1,1,256]{2,1,0:T(1,128)S(1)}, s32[1,1,256]{2,1,0:T(1,128)}, u32[]{:S(2)}) copy-start(s32[1,1,256]{2,1,0:T(1,128)} %param.7) | copy-start | bytes 3076
  2.1 0.7 %copy-start.3 = (f32[1,1,256]{2,1,0:T(1,128)S(1)}, f32[1,1,256]{2,1,0:T(1,128)}, u32[]{:S(2)}) copy-start(f32[1,1,256]{2,1,0:T(1,128)} %param.8) | copy-start | bytes 3076
  2.8 0.7 %copy-start.4 = (f32[1,1,256]{2,1,0:T(1,128)S(1)}, f32[1,1,256]{2,1,0:T(1,128)}, u32[]{:S(2)}) copy-start(f32[1,1,256]{2,1,0:T(1,128)} %param.9) | copy-start | bytes 3076

commit v4 on v3

--- a/solution.py
+++ b/solution.py
@@ -336,7 +336,9 @@
         compiler_params=pltpu.CompilerParams(
             collective_id=0, has_side_effects=True, vmem_limit_bytes=24 << 20
         ),
-    )(prior, obs_column, obs_value, obs_precision)
+    )(*(pltpu.with_memory_space_constraint(x, pltpu.HBM) for x in (
+        prior, obs_column, obs_value, obs_precision
+    )))
 
 
 def analysis_kernel(

time: 43.5 us -> 38.6 us (0.89)
  the two profiles are of different devices: /device:TPU:1 before, /device:TPU:0 now
where the time goes in v4:
time: 38.6 us; the launch traced here: 38 us
  Pallas kernels  37.9 us (98%)
    pallas_call x1, Pallas kernels, forecast(): pl.pallas_call(functools.partial(forecast_kernel, lax.axis_size('gx'), la...  29.3 us
    pallas_call x1, Pallas kernels, analyse(): pl.pallas_call(functools.partial(analysis_kernel, geometry), out_shape=ja...  8.63 us

profile of v4, /device:TPU:0, one launch (start us, length us, event | category | flops | bytes accessed | tf_op | source)
XLA Modules:
  0.0 38.0 jit_solution(15461302835704051570)
XLA Ops:
  0.0 0.0 copy-start.1
  0.0 0.0 copy-start
  0.0 29.3 %shard_map.64 = (f32[6,8,64,128]{3,2,1,0:T(8,128)S(1)}, f32[9,64,256]{2,1,0:T(8,128)S(1)}, f32[9,8,256]{2,1,0:T(8,128)S(1)}) custom-call(f32[64,6,8,128]{3,2,1,0:T(8,128)} %bitcast.7, s32[1,256]{1,0:T(1,128)} %bitcast.8, f32[1,256]{1,0:T(1,128)} %bitcast.9, f32[1,256]{1,0:T(1,128)} %bitcast.10), custom_call_target="tpu_custom_call" | custom-call | tf_op jit(solution)/shard_map/pallas_call | solution.py:310
  29.3 0.0 copy-done.1
  29.3 0.0 copy-done
  29.3 8.6 %shard_map.65 = f32[64,6,8,128]{3,2,1,0:T(8,128)} custom-call(f32[6,8,64,128]{3,2,1,0:T(8,128)S(1)} %get-tuple-element.8.fields_ref, f32[9,64,256]{2,1,0:T(8,128)S(1)} %get-tuple-element.9.table_ref, f32[9,8,256]{2,1,0:T(8,128)S(1)} %get-tuple-element.10.extras_ref, s32[16,128]{1,0:T(8,128)S(1)} %bitcast.6, s32[1,16]{1,0:T(1,128)S(1)} %copy-done.1), custom_call_target="tpu_custom_call" | custom-call | tf_op jit(solution)/shard_map/pallas_call | solution.py:561
Async XLA Ops:
  0.0 29.3 %copy-start.1 = (s32[1,16]{1,0:T(1,128)S(1)}, s32[1,16]{1,0:T(1,128)}, u32[]{:S(2)}) copy-start(s32[1,16]{1,0:T(1,128)} %count_ref.1) | copy-start | bytes 196
  0.0 29.3 %copy-start = (s32[1,16,128]{2,1,0:T(8,128)S(1)}, s32[1,16,128]{2,1,0:T(8,128)}, u32[]{:S(2)}) copy-start(s32[1,16,128]{2,1,0:T(8,128)} %param.10) | copy-start | bytes 24580
